TPU v7x, 512 devices: a whole 4x8x8 slice. The times are simulated.
512 devices in a mesh: dom: 32 (over x, z), wide: 16 (over y, core).
Axes of the slice: x: 4, y: 8, z: 8, core: 2. Of those that a mesh axis runs over, the one named last changes fastest.
Arguments:
- features: bfloat16 [131072, 512], P(('dom', 'wide')), may hold values from -6 to 6
- w_self: bfloat16 [512, 512], replicated, may hold values from -0.25 to 0.25
- w_neigh: bfloat16 [512, 512], replicated, may hold values from -0.25 to 0.25
- boundary: int32 [512, 2, 64], P(('dom', 'wide')), may hold values from 0 to 255
- neighbors: int32 [131072, 16], P(('dom', 'wide')), may hold values from 0 to 384, as said below
- anchors: int32 [8192, 32], P(('dom', 'wide')), may hold values from 0 to 255
- negatives: int32 [8192, 32, 8], P(('dom', 'wide')), may hold values from 0 to 255
- positives: int32 [131072, 2], P(('dom', 'wide')), may hold values from 0 to 255
Outputs:
- embed: bfloat16 [131072, 512], P(('dom', 'wide'))
- embed_grad: bfloat16 [131072, 512], P(('dom', 'wide'))
Inputs may be any that keep to these rules, and one draw needn't show every extreme that they name: `neighbors`: each row has its live slots first, 1 to 16 of them; the first node of every partition has 16; slots after the live ones hold 384. `anchors`: rows of the own partition. `negatives`: rows of the own partition. `positives`: rows of the own partition.
All inputs are finite; a program needn't handle non-finite values.
Results may differ from a plain program's by a relative error of at most 0.0053.
Values may be sent and summed in bfloat16 or wider, within the bound.
No kernel may reach another device: no remote copies, remote signals or barrier semaphores. Data moves between devices by JAX's collectives and lax.ppermute only.
A program may use at most 64 MiB of HBM per device.

v0:
```python
import math

import jax
import jax.numpy as jnp
from jax import lax
from jax.sharding import PartitionSpec as P


def passed_along(block, axis, distance):
    devices = range(lax.axis_size(axis))
    route = [(i - distance, i) for i in devices if i - distance in devices]
    return lax.ppermute(block, axis, route)


def pick_rows(index, table):
    columns = jnp.arange(table.shape[0], dtype=jnp.int32)[None, :]
    onehot = (index.reshape(-1)[:, None] == columns).astype(table.dtype)
    return jnp.dot(onehot, table, preferred_element_type=jnp.float32).astype(table.dtype)


def spread_rows(index, weights, rows, node_dev):
    nodes = jnp.arange(node_dev, dtype=jnp.int32)[:, None]
    mixing = jnp.where(nodes == index.reshape(-1)[None, :], weights[None, :], 0.0)
    return jnp.dot(
        mixing,
        rows.astype(jnp.float32),
        precision=lax.Precision.HIGHEST,
        preferred_element_type=jnp.float32,
    )


def body(features, w_self, w_neigh, boundary, neighbors, anchors, negatives, positives):
    node_dev = features.shape[0]
    width = features.shape[1]
    scale = 1.0 / math.sqrt(width)
    lists = boundary[0]
    below = passed_along(pick_rows(lists[0], features), "dom", 1)
    above = passed_along(pick_rows(lists[1], features), "dom", -1)
    table = jnp.concatenate([features, below, above], axis=0)
    table_rows = table.shape[0]
    columns = jnp.arange(table_rows, dtype=jnp.int32)[None, :]
    counts = jnp.zeros((node_dev, table_rows), jnp.bfloat16)
    for slot in range(neighbors.shape[1]):
        counts = counts + (neighbors[:, slot : slot + 1] == columns).astype(jnp.bfloat16)
    degree = jnp.sum((neighbors < table_rows).astype(jnp.float32), axis=1)
    summed = jnp.dot(counts, table, preferred_element_type=jnp.float32)
    mean = (summed / degree[:, None]).astype(jnp.bfloat16)
    embed = (
        jnp.dot(features, w_self, preferred_element_type=jnp.float32)
        + jnp.dot(mean, w_neigh, preferred_element_type=jnp.float32)
    ).astype(jnp.bfloat16)
    peers = anchors.shape[0]
    anch = anchors.shape[1]
    fan = negatives.shape[2]
    a_rows = pick_rows(anchors, embed).reshape(peers, anch, width)
    own_rows = pick_rows(negatives, embed).reshape(peers, anch, fan, width)
    got = lax.all_to_all(a_rows, "wide", split_axis=0, concat_axis=0, tiled=True)
    coef = jax.nn.sigmoid(
        jnp.einsum("vad,vakd->vak", got, own_rows, preferred_element_type=jnp.float32) * scale
    )
    nodes = jnp.arange(node_dev, dtype=jnp.int32)[:, None, None]
    mixing = jnp.sum(
        jnp.where(
            nodes == negatives.reshape(1, peers * anch, fan),
            coef.reshape(1, peers * anch, fan),
            0.0,
        ),
        axis=2,
    )
    grad = jnp.dot(
        mixing,
        got.reshape(-1, width).astype(jnp.float32),
        precision=lax.Precision.HIGHEST,
        preferred_element_type=jnp.float32,
    )
    back = jnp.sum(coef[..., None] * own_rows.astype(jnp.float32), axis=2)
    anchor_terms = lax.all_to_all(back, "wide", split_axis=0, concat_axis=0, tiled=True)
    ones = jnp.ones((peers * anch,), jnp.float32)
    grad = grad + spread_rows(anchors, ones, anchor_terms.reshape(-1, width), node_dev)
    first = pick_rows(positives[:, 0], embed)
    second = pick_rows(positives[:, 1], embed)
    coef_pos = (
        jax.nn.sigmoid(
            jnp.einsum("nd,nd->n", first, second, preferred_element_type=jnp.float32) * scale
        )
        - 1.0
    )
    both_index = jnp.concatenate([positives[:, 0], positives[:, 1]], axis=0)
    both_coef = jnp.concatenate([coef_pos, coef_pos], axis=0)
    both_rows = jnp.concatenate([second, first], axis=0)
    grad = grad + spread_rows(both_index, both_coef, both_rows, node_dev)
    return (embed, grad.astype(jnp.bfloat16))


def solution(mesh):
    return jax.shard_map(
        body,
        mesh=mesh,
        in_specs=(
            P(("dom", "wide"), None),
            P(),
            P(),
            P(("dom", "wide"), None, None),
            P(("dom", "wide"), None),
            P(("dom", "wide"), None),
            P(("dom", "wide"), None, None),
            P(("dom", "wide"), None),
        ),
        out_specs=(P(("dom", "wide"), None), P(("dom", "wide"), None)),
        check_vma=False,
    )
```

profile of v0, /device:TPU:7, one launch (start us, length us, event | category | flops | bytes accessed | tf_op | source)
XLA Modules:
  0.0 91.5 jit_solution(342744891424264483)
XLA Ops:
  0.6 0.8 slice_bitcast_fusion.1
  1.4 1.1 %convolution_convert_fusion.5 = bf16[64,512]{1,0:T(8,128)(2,1)S(1)} fusion(bf16[256,512]{1,0:T(8,128)(2,1)} %param.8, s32[64]{0:T(128)S(1)} %get-tuple-element.20), kind=kOutput, calls=%fused_computation.17 | convolution fusion | flops 16826368 | bytes 327936 | tf_op jit(solution)/shard_map/dot_general | solution.py:18
  2.6 4.0 %collective-permute-start = (bf16[64,512]{1,0:T(8,128)(2,1)S(1)}, bf16[64,512]{1,0:T(8,128)(2,1)S(1)}, u32[]{:S(2)}, u32[]{:S(2)}) collective-permute-start(bf16[64,512]{1,0:T(8,128)(2,1)S(1)} %convolution_convert_fusion.5), channel_id=1, source_target_pairs={{0,16},{16,32},{32,48},{48,64},{64,80},{80,96},{96,112},{112,128},... | collective-permute-start | bytes 196616 | tf_op jit(solution)/shard_map/ppermute | solution.py:12
  6.6 1.2 %convolution_convert_fusion.4 = bf16[64,512]{1,0:T(8,128)(2,1)S(1)} fusion(bf16[256,512]{1,0:T(8,128)(2,1)} %param.8, s32[64]{0:T(128)S(1)} %get-tuple-element.21), kind=kOutput, calls=%fused_computation.16 | convolution fusion | flops 16826368 | bytes 327936 | tf_op jit(solution)/shard_map/dot_general | solution.py:18
  7.7 8.9 %collective-permute-start.1 = (bf16[64,512]{1,0:T(8,128)(2,1)S(1)}, bf16[64,512]{1,0:T(8,128)(2,1)S(1)}, u32[]{:S(2)}, u32[]{:S(2)}) collective-permute-start(bf16[64,512]{1,0:T(8,128)(2,1)S(1)} %convolution_convert_fusion.4), channel_id=1, source_target_pairs={{16,0},{32,16},{48,32},{64,48},{80,64},{96,80},{112,96},{128,112},... | collective-permute-start | bytes 196616 | tf_op jit(solution)/shard_map/ppermute | solution.py:12
  16.6 1.0 %fusion.141 = (s32[256,1]{0,1:T(1,128)S(1)}, s32[256,1]{0,1:T(1,128)S(1)}, s32[256,1]{0,1:T(1,128)S(1)}, s32[256,1]{0,1:T(1,128)S(1)}, s32[256,1]{0,1:T(1,128)S(...) fusion(s32[256,16]{0,1:T(8,128)} %param.12), kind=kLoop, calls=%fused_computation.131 | loop fusion | bytes 32768 | tf_op jit(solution)/shard_map/slice | solution.py:44
  17.6 1.2 %fusion.143 = f32[256,512]{1,0:T(8,128)S(1)} fusion(bf16[256,512]{1,0:T(8,128)(2,1)} %param.8, bf16[512,512]{1,0:T(8,128)(2,1)S(1)} %copy-done), kind=kOutput, calls=%fused_computation.133 | convolution fusion | flops 134217728 | bytes 1310720 | tf_op jit(solution)/shard_map/dot_general | solution.py:49
  18.9 0.8 eq.443
  19.6 0.7 convert_reduce_fusion
  20.4 2.3 %fusion.2 = bf16[256,512]{1,0:T(8,128)(2,1)S(1)} fusion(f32[256,512]{1,0:T(8,128)S(1)} %fusion.143, bf16[512,512]{1,0:T(8,128)(2,1)} %param.10, bf16[64,512]{1,0:T(8,128)(2,1)S(1)} %collective-permute-done.1, bf16[64,512]{1,0:T(8,128)(2,1)S(1)} %collective-permute-done, bf16[256,512]{1,0:T(8,128)(2,1)} %param.8, f32[256]{0:T(256)S(1)} %convert_reduce_fusion, ...), kind=kOutput, calls=%fused_computation.11 | convolution fusion | flops 242876416 | bytes 1721344 | tf_op jit(solution)/shard_map/dot_general | solution.py:50
  22.7 1.1 %convolution_convert_fusion.1 = bf16[512,512]{1,0:T(8,128)(2,1)} fusion(bf16[256,512]{1,0:T(8,128)(2,1)S(1)} %fusion.2, s32[512]{0:T(512)S(1)} %eq.443), kind=kOutput, calls=%fused_computation.6 | convolution fusion | flops 134610944 | bytes 788480 | tf_op jit(solution)/shard_map/dot_general | solution.py:18
  23.9 8.1 %all-to-all-start = ((bf16[16,32,512]{2,1,0:T(8,128)(2,1)}), bf16[16,32,512]{2,1,0:T(8,128)(2,1)S(1)}, u32[]{:S(2)}, u32[]{:S(2)}) async-start(bf16[16,32,512]{2,1,0:T(8,128)(2,1)} %bitcast.18), calls=%async_computation | async-start | bytes 1048576 | tf_op jit(solution)/shard_map/all_to_all | solution.py:57
  32.2 2.9 %convolution_convert_fusion = bf16[4096,512]{1,0:T(8,128)(2,1)} fusion(bf16[256,512]{1,0:T(8,128)(2,1)S(1)} %fusion.2, s32[4096]{0:T(1024)S(1)} %eq.447), kind=kOutput, calls=%fused_computation.1 | convolution fusion | flops 1076887552 | bytes 4472832 | tf_op jit(solution)/shard_map/dot_general | solution.py:18
  35.1 14.1 %all-to-all-done = bf16[16,32,512]{2,1,0:T(8,128)(2,1)S(1)} async-done(((bf16[16,32,512]{2,1,0:T(8,128)(2,1)}), bf16[16,32,512]{2,1,0:T(8,128)(2,1)S(1)}, u32[]{:S(2)}, u32[]{:S(2)}) %all-to-all-start) | async-done | bytes 524320 | tf_op jit(solution)/shard_map/all_to_all | solution.py:57
  49.2 4.0 %fusion.5 = f32[16,32,1,8]{3,2,1,0:T(1,128)S(1)} fusion(bf16[16,32,8,512]{3,2,1,0:T(8,128)(2,1)} %bitcast.55, bf16[16,32,512,1]{2,1,0,3:T(8,128)(2,1)S(1)} %bitcast.57), kind=kOutput, calls=%fused_computation.18 | convolution fusion | flops 4194304 | bytes 4734976 | tf_op jit(solution)/shard_map/vad,vakd->vak/dot_general | solution.py:59
  53.5 5.3 %multiply_reduce_fusion = f32[16,32,512]{2,1,0:T(8,128)} fusion(f32[16,32,8]{2,1,0:T(8,128)S(1)} %copy.22, bf16[4096,512]{1,0:T(8,128)(2,1)} %convolution_convert_fusion), kind=kLoop, calls=%fused_computation | loop fusion | flops 6029312 | bytes 5259264 | tf_op jit(solution)/shard_map/reduce_sum | solution.py:76
  58.8 3.5 %all-to-all-start.1 = ((f32[16,32,512]{2,1,0:T(8,128)}), f32[16,32,512]{2,1,0:T(8,128)S(1)}, u32[]{:S(2)}, u32[]{:S(2)}) async-start(f32[16,32,512]{2,1,0:T(8,128)} %multiply_reduce_fusion), calls=%async_computation.1 | async-start | bytes 2097152 | tf_op jit(solution)/shard_map/all_to_all | solution.py:77
  62.5 0.3 convolution_convert_fusion.2
  62.8 0.4 fusion.11
  63.1 0.6 fusion.7
  63.9 1.5 %select_reduce_fusion = f32[256,512]{1,0:T(8,128)S(1)} fusion(f32[512,8]{0,1:T(8,128)S(1)} %broadcast_in_dim.46, s32[512,8]{0,1:T(8,128)S(1)} %eq.440), kind=kLoop, calls=%fused_computation.2 | loop fusion | flops 3014656 | bytes 557056 | tf_op jit(solution)/shard_map/reduce_sum | solution.py:62
  65.3 0.6 fusion.144
  65.9 23.7 %all-to-all-done.1 = f32[16,32,512]{2,1,0:T(8,128)S(1)} async-done(((f32[16,32,512]{2,1,0:T(8,128)}), f32[16,32,512]{2,1,0:T(8,128)S(1)}, u32[]{:S(2)}, u32[]{:S(2)}) %all-to-all-start.1) | async-done | bytes 1048608 | tf_op jit(solution)/shard_map/all_to_all | solution.py:77
  89.7 1.8 %fusion.3 = bf16[256,512]{1,0:T(8,128)(2,1)} fusion(f32[256,512]{1,0:T(8,128)S(1)} %fusion.7, f32[256,512]{1,0:T(8,128)S(1)} %fusion.144, f32[512,512]{1,0:T(8,128)S(1)} %bitcast.56, s32[512]{0:T(512)S(1)} %eq.443), kind=kOutput, calls=%fused_computation.12 | convolution fusion | flops 805961728 | bytes 2361344 | tf_op jit(solution)/shard_map/dot_general | solution.py:24
  (23 shorter events, 0.8 us)
Async XLA Ops:
  0.6 17.0 %copy-start = (bf16[512,512]{1,0:T(8,128)(2,1)S(1)}, bf16[512,512]{1,0:T(8,128)(2,1)}, u32[]{:S(2)}) copy-start(bf16[512,512]{1,0:T(8,128)(2,1)} %param.9) | copy-start | bytes 1572868
  2.6 17.8 %collective-permute-start = (bf16[64,512]{1,0:T(8,128)(2,1)S(1)}, bf16[64,512]{1,0:T(8,128)(2,1)S(1)}, u32[]{:S(2)}, u32[]{:S(2)}) collective-permute-start(bf16[64,512]{1,0:T(8,128)(2,1)S(1)} %convolution_convert_fusion.5), channel_id=1, source_target_pairs={{0,16},{16,32},{32,48},{48,64},{64,80},{80,96},{96,112},{112,128},... | collective-permute-start | bytes 196616 | tf_op jit(solution)/shard_map/ppermute | solution.py:12
  7.7 12.7 %collective-permute-start.1 = (bf16[64,512]{1,0:T(8,128)(2,1)S(1)}, bf16[64,512]{1,0:T(8,128)(2,1)S(1)}, u32[]{:S(2)}, u32[]{:S(2)}) collective-permute-start(bf16[64,512]{1,0:T(8,128)(2,1)S(1)} %convolution_convert_fusion.4), channel_id=1, source_target_pairs={{16,0},{32,16},{48,32},{64,48},{80,64},{96,80},{112,96},{128,112},... | collective-permute-start | bytes 196616 | tf_op jit(solution)/shard_map/ppermute | solution.py:12
  20.4 11.6 %copy-start.2 = (s32[16,32,8]{1,2,0:T(8,128)S(1)}, s32[16,32,8]{1,2,0:T(8,128)}, u32[]{:S(2)}) copy-start(s32[16,32,8]{1,2,0:T(8,128)} %param.14) | copy-start | bytes 49156
  22.7 40.0 %copy-start.1 = (bf16[256,512]{1,0:T(8,128)(2,1)}, bf16[256,512]{1,0:T(8,128)(2,1)S(1)}, u32[]{:S(2)}) copy-start(bf16[256,512]{1,0:T(8,128)(2,1)S(1)} %fusion.2) | copy-start | bytes 786436
  23.9 25.3 %all-to-all-start = ((bf16[16,32,512]{2,1,0:T(8,128)(2,1)}), bf16[16,32,512]{2,1,0:T(8,128)(2,1)S(1)}, u32[]{:S(2)}, u32[]{:S(2)}) async-start(bf16[16,32,512]{2,1,0:T(8,128)(2,1)} %bitcast.18), calls=%async_computation | async-start | bytes 1048576 | tf_op jit(solution)/shard_map/all_to_all | solution.py:57
  53.3 9.1 %copy-start.3 = (s32[256,2]{0,1:T(2,128)S(1)}, s32[256,2]{0,1:T(2,128)}, u32[]{:S(2)}) copy-start(s32[256,2]{0,1:T(2,128)} %param.15) | copy-start | bytes 6148
  58.8 30.9 %all-to-all-start.1 = ((f32[16,32,512]{2,1,0:T(8,128)}), f32[16,32,512]{2,1,0:T(8,128)S(1)}, u32[]{:S(2)}, u32[]{:S(2)}) async-start(f32[16,32,512]{2,1,0:T(8,128)} %multiply_reduce_fusion), calls=%async_computation.1 | async-start | bytes 2097152 | tf_op jit(solution)/shard_map/all_to_all | solution.py:77
where the time goes:
time: 92.1 us; the launch traced here: 91.5 us
  waiting for transfers between devices  37.8 us (41%)
  starting transfers between devices  24.5 us (27%)
  matrix products  17.5 us (19%)
  other arithmetic  7.53 us (8%)
  local copies, waits for them, and re-layouts  3.32 us (4%)
    all_to_all x1, waiting for transfers between devices, body(): lax.all_to_all(back, 'wide', split_axis=0, concat_axis=0, tiled=True)  23.7 us
    all_to_all x1, waiting for transfers between devices, body(): lax.all_to_all(a_rows, 'wide', split_axis=0, concat_axis=0, tiled=True)  14.1 us
    ppermute x2, starting transfers between devices, passed_along(): return lax.ppermute(block, axis, route)  12.9 us
    all_to_all x1, starting transfers between devices, body(): lax.all_to_all(a_rows, 'wide', split_axis=0, concat_axis=0, tiled=True)  8.07 us
    dot_general x6, matrix products, pick_rows(): jnp.dot(onehot, table, preferred_element_type=jnp.float32)  6.93 us
    reduce_sum x1, other arithmetic, body(): back = jnp.sum(coef[..., None] * own_rows.astype(jnp.float32), axis=2)  5.26 us
    dot_general x1, matrix products, body(): jnp.einsum('vad,vakd->vak', got, own_rows, preferred_element_type=jnp.flo...  4.03 us
    all_to_all x1, starting transfers between devices, body(): lax.all_to_all(back, 'wide', split_axis=0, concat_axis=0, tiled=True)  3.55 us
  transfers between devices with their start and end apart: 4, of which 2 were waited for; matrix products, arithmetic and copies ran while one was open for 13% of the time, Pallas kernels for 0%

commit v1 on v0

v1 whole, which is shorter than its diff:
```python
import functools
import math

import jax
import jax.numpy as jnp
from jax import lax
from jax.experimental import pallas as pl
from jax.experimental.pallas import tpu as pltpu
from jax.sharding import PartitionSpec as P

F32 = jnp.float32
BF16 = jnp.bfloat16


def shape(dims, dtype):
    return pltpu.VMEM(dims, dtype)


def call(kernel, outs, *operands, from_hbm=0, **static):
    spaces = [pltpu.HBM] * from_hbm + [pltpu.VMEM] * (len(operands) - from_hbm)
    return pl.pallas_call(
        functools.partial(kernel, **static) if static else kernel,
        out_shape=outs,
        in_specs=[pl.BlockSpec(memory_space=space) for space in spaces],
        out_specs=[pl.BlockSpec(memory_space=pltpu.VMEM)] * len(outs),
        scratch_shapes=[pltpu.SemaphoreType.DMA((from_hbm,))] if from_hbm else [],
        compiler_params=pltpu.CompilerParams(vmem_limit_bytes=4 * 2**20),
        name=kernel.__name__,
    )(*[pltpu.with_memory_space_constraint(x, space) for x, space in zip(operands, spaces)])


def fetch(pairs, arrived):
    copies = [pltpu.make_async_copy(a, b, arrived.at[n]) for n, (a, b) in enumerate(pairs)]
    for copy in copies:
        copy.start()
    return copies


def dot(a, b):
    return jnp.dot(a, b, preferred_element_type=F32)


def dot_nt(a, b):
    return lax.dot_general(a, b, (((1,), (1,)), ((), ())), preferred_element_type=F32)


def dot_tn(a, b):
    return lax.dot_general(a, b, (((0,), (0,)), ((), ())), preferred_element_type=F32)


def column_counts(columns, width, offset=0):
    rows, slots = columns.shape
    lanes = lax.broadcasted_iota(jnp.int32, (rows, width), 1) + offset
    total = jnp.zeros((rows, width), F32)
    for slot in range(slots):
        total = total + jnp.where(columns[:, slot : slot + 1] == lanes, 1.0, 0.0)
    return total


def row_counts(rows, height):
    slots, width = rows.shape
    levels = lax.broadcasted_iota(jnp.int32, (height, width), 0)
    total = jnp.zeros((height, width), F32)
    for slot in range(slots):
        total = total + jnp.where(rows[slot : slot + 1, :] == levels, 1.0, 0.0)
    return total


def head_kernel(*refs):
    fetched = 4
    held, (up_ref, down_ref, arrived) = refs[fetched : 2 * fetched], refs[2 * fetched :]
    copies = fetch(zip(refs[:fetched], held), arrived)
    lists_ref, features_ref = held[:2]
    copies[0].wait()
    nodes = features_ref.shape[0]
    onehots = [row_counts(lists_ref[0, side : side + 1, :], nodes).astype(BF16) for side in range(2)]
    copies[1].wait()
    for onehot, out in zip(onehots, (up_ref, down_ref)):
        out[...] = dot_tn(onehot, features_ref[...]).astype(BF16)
    for copy in copies[2:]:
        copy.wait()


def own_kernel(*refs):
    fetched = 4
    given, (features_ref, neighbors_ref, anchors_ref) = refs[:fetched], refs[fetched : fetched + 3]
    held = refs[fetched + 3 : 2 * fetched + 3]
    own_ref, summed_ref, counts_ref, degree_ref, pick_ref, arrived = refs[2 * fetched + 3 :]
    copies = fetch(zip(given, held), arrived)
    features = features_ref[...]
    nodes = features.shape[0]
    edge = counts_ref.shape[1]
    counts = column_counts(neighbors_ref[...].T, nodes + edge)
    degree_ref[...] = jnp.sum(counts, axis=1, keepdims=True)
    counts = counts.astype(BF16)
    counts_ref[...] = counts[:, nodes:]
    summed_ref[...] = dot(counts[:, :nodes], features)
    slots = jnp.concatenate([anchors_ref[j : j + 1, :] for j in range(anchors_ref.shape[0])], axis=1)
    pick_ref[...] = column_counts(slots.T, nodes).astype(BF16)
    copies[0].wait()
    own_ref[...] = dot(features, held[0][...])
    for copy in copies[1:]:
        copy.wait()


def embed_kernel(below_ref, above_ref, counts_ref, degree_ref, summed_ref, own_ref, w_neigh_ref, pick_ref, embed_ref, rows_ref):
    rows = below_ref.shape[0]
    summed = summed_ref[...] + dot(counts_ref[:, :rows], below_ref[...]) + dot(counts_ref[:, rows:], above_ref[...])
    mean = (summed / degree_ref[...]).astype(BF16)
    embed = (own_ref[...] + dot(mean, w_neigh_ref[...])).astype(BF16)
    embed_ref[...] = embed
    rows_ref[...] = dot(pick_ref[...], embed).astype(BF16)


def local_kernel(negatives_ref, positives_ref, anchors_ref, embed_ref, live_ref, spread_ref, grad_ref, *, scale):
    embed = embed_ref[...]
    nodes = embed.shape[0]
    peers = negatives_ref.shape[0]
    slots = jnp.concatenate([negatives_ref[j] for j in range(peers)], axis=1)
    live_ref[...] = column_counts(slots.T, nodes).astype(BF16)
    anchors = jnp.concatenate([anchors_ref[j : j + 1, :] for j in range(peers)], axis=1)
    spread_ref[...] = row_counts(anchors, nodes).astype(BF16)
    first = row_counts(positives_ref[0:1, :], nodes).astype(BF16)
    second = row_counts(positives_ref[1:2, :], nodes).astype(BF16)
    pairs = dot_nt(first, second) + dot_nt(second, first)
    weight = (jax.nn.sigmoid(dot_nt(embed, embed) * scale) - 1.0) * pairs
    grad_ref[...] = dot(weight.astype(BF16), embed)


def score_kernel(got_ref, embed_ref, live_ref, weight_ref, back_ref, *, scale):
    embed = embed_ref[...]
    weight = jax.nn.sigmoid(dot_nt(got_ref[...], embed) * scale) * live_ref[...].astype(F32)
    weight = weight.astype(BF16)
    weight_ref[...] = weight
    back_ref[...] = dot(weight, embed).astype(BF16)


def owner_kernel(weight_ref, got_ref, grad_ref, out_ref):
    out_ref[...] = grad_ref[...] + dot_tn(weight_ref[...], got_ref[...])


def final_kernel(spread_ref, terms_ref, grad_ref, out_ref):
    out_ref[...] = (grad_ref[...] + dot(spread_ref[...], terms_ref[...])).astype(BF16)


def passed_along(block, axis, distance):
    devices = range(lax.axis_size(axis))
    route = [(i - distance, i) for i in devices if i - distance in devices]
    return lax.ppermute(block, axis, route)


def exchanged(rows, peers):
    block = rows.reshape(peers, -1, rows.shape[1])
    return lax.all_to_all(block, "wide", split_axis=0, concat_axis=0, tiled=True).reshape(rows.shape)


def body(features, w_self, w_neigh, boundary, neighbors, anchors, negatives, positives):
    nodes, width = features.shape
    scale = 1.0 / math.sqrt(width)
    peers, anch = anchors.shape
    slots = peers * anch
    edge = boundary.shape[2]
    given = (boundary, features, neighbors.T, anchors)
    _, features, neighbors, anchors, up, down = call(
        head_kernel,
        [shape(x.shape, x.dtype) for x in given] + [shape((edge, width), BF16)] * 2,
        *given,
        from_hbm=len(given),
    )
    below = passed_along(up, "dom", 1)
    above = passed_along(down, "dom", -1)
    given = (w_self, w_neigh, negatives.transpose(0, 2, 1), positives.T)
    _, w_neigh, negatives, positives, own, summed, counts, degree, pick = call(
        own_kernel,
        [shape(x.shape, x.dtype) for x in given]
        + [
            shape((nodes, width), F32),
            shape((nodes, width), F32),
            shape((nodes, 2 * edge), BF16),
            shape((nodes, 1), F32),
            shape((slots, nodes), BF16),
        ],
        *given,
        features,
        neighbors,
        anchors,
        from_hbm=len(given),
    )
    embed, rows = call(
        embed_kernel,
        [shape((nodes, width), BF16), shape((slots, width), BF16)],
        below,
        above,
        counts,
        degree,
        summed,
        own,
        w_neigh,
        pick,
    )
    got = exchanged(rows, peers)
    live, spread, grad = call(
        local_kernel,
        [shape((slots, nodes), BF16), shape((nodes, slots), BF16), shape((nodes, width), F32)],
        negatives,
        positives,
        anchors,
        embed,
        scale=scale,
    )
    weight, back = call(
        score_kernel,
        [shape((slots, nodes), BF16), shape((slots, width), BF16)],
        got,
        embed,
        live,
        scale=scale,
    )
    terms = exchanged(back, peers)
    [grad] = call(owner_kernel, [shape((nodes, width), F32)], weight, got, grad)
    [out] = call(final_kernel, [shape((nodes, width), BF16)], spread, terms, grad)
    return (embed, out)


def solution(mesh):
    split = P(("dom", "wide"))
    return jax.shard_map(
        body,
        mesh=mesh,
        in_specs=(split, P(), P(), split, split, split, split, split),
        out_specs=(split, split),
        check_vma=False,
    )
```

time: 92.1 us -> 67.6 us (0.73)
  matrix products: 17.5 us -> 0 us
  Pallas kernels: 0 us -> 8.91 us
  other arithmetic: 7.53 us -> 0 us
  waiting for transfers between devices: 37.8 us -> 31.9 us
  local copies, waits for them, and re-layouts: 3.32 us -> 1.41 us
    dot_general x12 -> x0, matrix products: 17.5 us -> none  [the longest x6 6.93 us: pick_rows(): jnp.dot(onehot, table, preferred_element_type=jnp.float32)]
    pallas_call x0 -> x7, Pallas kernels: none -> 8.91 us  [call(): pl.pallas_call(functools.partial(kernel, **static) if static else kernel,...]
    reduce_sum x3 -> x0, other arithmetic: 7.47 us -> none  [the longest x1 5.26 us: body(): back = jnp.sum(coef[..., None] * own_rows.astype(jnp.float32), axis=2)]
    all_to_all x2, waiting for transfers between devices: 37.8 us -> 31.9 us  [exchanged(): lax.all_to_all(block, 'wide', split_axis=0, concat_axis=0, tiled=True)]
    eq x4 -> x0, local copies, waits for them, and re-layouts: 1.77 us -> none  [the longest x3 1.68 us: pick_rows(): onehot = (index.reshape(-1)[:, None] == columns).astype(table.dtype)]
    unnamed x10 -> x2, local copies, waits for them, and re-layouts: 0.16 us -> 1.41 us
    slice x2 -> x0, local copies, waits for them, and re-layouts: 1.02 us -> none  [the longest x1 1.02 us: body(): neighbors[:, slot:slot + 1] == columns]
  transfers between devices with their start and end apart: 4 -> 4, of which waited for: 2 -> 2; matrix products, arithmetic and copies ran while one was open for 13% -> 1% of each run, Pallas kernels for 0% -> 6%
where the time goes in v1:
time: 67.6 us; the launch traced here: 67.3 us
  waiting for transfers between devices  31.9 us (47%)
  starting transfers between devices  24.4 us (36%)
  Pallas kernels  8.91 us (13%)
  local copies, waits for them, and re-layouts  1.41 us (2%)
  between operations  0.71 us (1%)
    all_to_all x2, waiting for transfers between devices, exchanged(): lax.all_to_all(block, 'wide', split_axis=0, concat_axis=0, tiled=True)  31.9 us
    ppermute x2, starting transfers between devices, passed_along(): return lax.ppermute(block, axis, route)  12.9 us
    all_to_all x2, starting transfers between devices, exchanged(): lax.all_to_all(block, 'wide', split_axis=0, concat_axis=0, tiled=True)  11.5 us
    pallas_call x7, Pallas kernels, call(): pl.pallas_call(functools.partial(kernel, **static) if static else kernel,...  8.91 us
    unnamed x2, local copies, waits for them, and re-layouts  1.41 us
  transfers between devices with their start and end apart: 4, of which 2 were waited for; matrix products, arithmetic and copies ran while one was open for 1% of the time, Pallas kernels for 6%

profile of v1, /device:TPU:7, one launch (start us, length us, event | category | flops | bytes accessed | tf_op | source)
XLA Modules:
  0.0 67.3 jit_solution(12201238012032934761)
XLA Ops:
  0.6 1.8 %head_kernel.1 = (s32[1,2,64]{2,1,0:T(2,128)}, bf16[256,512]{1,0:T(8,128)(2,1)S(1)}, s32[16,256]{1,0:T(8,128)S(1)}, s32[16,32]{1,0:T(8,128)S(1)}, bf16[64,512]{1...) custom-call(s32[1,2,64]{2,1,0:T(2,128)} %refs_0_.2, bf16[256,512]{1,0:T(8,128)(2,1)} %refs_1_.2, s32[16,256]{1,0:T(8,128)} %bitcast.11, ...), custom_call_target="tpu_custom_call" | custom-call | tf_op jit(solution)/shard_map/head_kernel/pallas_call | solution.py:21
  2.4 4.0 %collective-permute-start = (bf16[64,512]{1,0:T(8,128)(2,1)S(1)}, bf16[64,512]{1,0:T(8,128)(2,1)S(1)}, u32[]{:S(2)}, u32[]{:S(2)}) collective-permute-start(bf16[64,512]{1,0:T(8,128)(2,1)S(1)} %get-tuple-element.22), channel_id=1, source_target_pairs={{0,16},{16,32},{32,48},{48,64},{64,80},{80,96},{96,112},{112,128},... | collective-permute-start | bytes 196616 | tf_op jit(solution)/shard_map/ppermute | solution.py:149
  6.4 8.9 %collective-permute-start.1 = (bf16[64,512]{1,0:T(8,128)(2,1)S(1)}, bf16[64,512]{1,0:T(8,128)(2,1)S(1)}, u32[]{:S(2)}, u32[]{:S(2)}) collective-permute-start(bf16[64,512]{1,0:T(8,128)(2,1)S(1)} %get-tuple-element.23), channel_id=1, source_target_pairs={{16,0},{32,16},{48,32},{64,48},{80,64},{96,80},{112,96},{128,112},... | collective-permute-start | bytes 196616 | tf_op jit(solution)/shard_map/ppermute | solution.py:149
  15.3 2.4 %own_kernel.1 = (bf16[512,512]{1,0:T(8,128)(2,1)}, bf16[512,512]{1,0:T(8,128)(2,1)S(1)}, s32[16,8,32]{2,1,0:T(8,128)S(1)}, s32[2,256]{1,0:T(2,128)S(1)}, f32[256...) custom-call(bf16[512,512]{1,0:T(8,128)(2,1)} %refs_0_.3, ...), custom_call_target="tpu_custom_call" | custom-call | tf_op jit(solution)/shard_map/own_kernel/pallas_call | solution.py:21
  17.7 0.0 collective-permute-done.below_ref
  17.7 0.0 collective-permute-done.1.above_ref
  17.7 1.6 %embed_kernel.1 = (bf16[256,512]{1,0:T(8,128)(2,1)S(1)}, bf16[512,512]{1,0:T(8,128)(2,1)}) custom-call(bf16[64,512]{1,0:T(8,128)(2,1)S(1)} %collective-permute-done.below_ref, bf16[64,512]{1,0:T(8,128)(2,1)S(1)} %collective-permute-done.1.above_ref, bf16[256,128]{1,0:T(8,128)(2,1)S(1)} %get-tuple-element.27.counts_ref, ...), custom_call_target="tpu_custom_call" | custom-call | tf_op jit(solution)/shard_map/embed_kernel/pallas_call | solution.py:21
  19.3 8.1 %all-to-all-start = ((bf16[16,32,512]{2,1,0:T(8,128)(2,1)}), bf16[16,32,512]{2,1,0:T(8,128)(2,1)S(1)}, u32[]{:S(2)}, u32[]{:S(2)}) async-start(bf16[16,32,512]{2,1,0:T(8,128)(2,1)} %bitcast.3), calls=%async_computation | async-start | bytes 1048576 | tf_op jit(solution)/shard_map/all_to_all | solution.py:154
  27.4 1.0 %local_kernel.1 = (bf16[512,256]{1,0:T(8,128)(2,1)S(1)}, bf16[256,512]{1,0:T(8,128)(2,1)S(1)}, f32[256,512]{1,0:T(8,128)S(1)}) custom-call(s32[16,8,32]{2,1,0:T(8,128)S(1)} %get-tuple-element.34.negatives_ref, s32[2,256]{1,0:T(2,128)S(1)} %get-tuple-element.35.positives_ref, s32[16,32]{1,0:T(8,128)S(1)} %get-tuple-element.26.refs_6_.anchors_ref, ...), custom_call_target="tpu_custom_call" | custom-call | tf_op jit(solution)/shard_map/local_kernel/pallas_call | solution.py:21
  28.4 16.2 %all-to-all-done = bf16[16,32,512]{2,1,0:T(8,128)(2,1)S(1)} async-done(((bf16[16,32,512]{2,1,0:T(8,128)(2,1)}), bf16[16,32,512]{2,1,0:T(8,128)(2,1)S(1)}, u32[]{:S(2)}, u32[]{:S(2)}) %all-to-all-start) | async-done | bytes 524320 | tf_op jit(solution)/shard_map/all_to_all | solution.py:154
  44.6 1.5 %score_kernel.1 = (bf16[512,256]{1,0:T(8,128)(2,1)S(1)}, bf16[512,512]{1,0:T(8,128)(2,1)}) custom-call(bf16[512,512]{1,0:T(8,128)(2,1)S(1)} %bitcast.7, bf16[256,512]{1,0:T(8,128)(2,1)S(1)} %get-tuple-element.42.embed_ref, bf16[512,256]{1,0:T(8,128)(2,1)S(1)} %get-tuple-element.38.live_ref), custom_call_target="tpu_custom_call" | custom-call | tf_op jit(solution)/shard_map/score_kernel/pallas_call | solution.py:21
  46.1 3.5 %all-to-all-start.1 = ((bf16[16,32,512]{2,1,0:T(8,128)(2,1)}), bf16[16,32,512]{2,1,0:T(8,128)(2,1)S(1)}, u32[]{:S(2)}, u32[]{:S(2)}) async-start(bf16[16,32,512]{2,1,0:T(8,128)(2,1)} %bitcast.5), calls=%async_computation.1 | async-start | bytes 1048576 | tf_op jit(solution)/shard_map/all_to_all | solution.py:154
  49.6 0.7 %copy.10 = bf16[256,512]{1,0:T(8,128)(2,1)} copy(bf16[256,512]{1,0:T(8,128)(2,1)S(1)} %get-tuple-element.42.embed_ref) | data formatting | bytes 524288
  50.3 0.3 owner_kernel.1.grad_ref
  50.6 15.7 %all-to-all-done.1 = bf16[16,32,512]{2,1,0:T(8,128)(2,1)S(1)} async-done(((bf16[16,32,512]{2,1,0:T(8,128)(2,1)}), bf16[16,32,512]{2,1,0:T(8,128)(2,1)S(1)}, u32[]{:S(2)}, u32[]{:S(2)}) %all-to-all-start.1) | async-done | bytes 524320 | tf_op jit(solution)/shard_map/all_to_all | solution.py:154
  66.3 0.3 final_kernel.1
  66.6 0.7 %copy.11 = bf16[256,512]{1,0:T(8,128)(2,1)} copy(bf16[256,512]{1,0:T(8,128)(2,1)S(1)} %final_kernel.1) | data formatting | bytes 524288
Async XLA Ops:
  2.4 15.3 %collective-permute-start = (bf16[64,512]{1,0:T(8,128)(2,1)S(1)}, bf16[64,512]{1,0:T(8,128)(2,1)S(1)}, u32[]{:S(2)}, u32[]{:S(2)}) collective-permute-start(bf16[64,512]{1,0:T(8,128)(2,1)S(1)} %get-tuple-element.22), channel_id=1, source_target_pairs={{0,16},{16,32},{32,48},{48,64},{64,80},{80,96},{96,112},{112,128},... | collective-permute-start | bytes 196616 | tf_op jit(solution)/shard_map/ppermute | solution.py:149
  6.4 11.3 %collective-permute-start.1 = (bf16[64,512]{1,0:T(8,128)(2,1)S(1)}, bf16[64,512]{1,0:T(8,128)(2,1)S(1)}, u32[]{:S(2)}, u32[]{:S(2)}) collective-permute-start(bf16[64,512]{1,0:T(8,128)(2,1)S(1)} %get-tuple-element.23), channel_id=1, source_target_pairs={{16,0},{32,16},{48,32},{64,48},{80,64},{96,80},{112,96},{128,112},... | collective-permute-start | bytes 196616 | tf_op jit(solution)/shard_map/ppermute | solution.py:149
  19.3 25.3 %all-to-all-start = ((bf16[16,32,512]{2,1,0:T(8,128)(2,1)}), bf16[16,32,512]{2,1,0:T(8,128)(2,1)S(1)}, u32[]{:S(2)}, u32[]{:S(2)}) async-start(bf16[16,32,512]{2,1,0:T(8,128)(2,1)} %bitcast.3), calls=%async_computation | async-start | bytes 1048576 | tf_op jit(solution)/shard_map/all_to_all | solution.py:154
  46.1 20.2 %all-to-all-start.1 = ((bf16[16,32,512]{2,1,0:T(8,128)(2,1)}), bf16[16,32,512]{2,1,0:T(8,128)(2,1)S(1)}, u32[]{:S(2)}, u32[]{:S(2)}) async-start(bf16[16,32,512]{2,1,0:T(8,128)(2,1)} %bitcast.5), calls=%async_computation.1 | async-start | bytes 1048576 | tf_op jit(solution)/shard_map/all_to_all | solution.py:154

commit v2 on v1

--- a/solution.py
+++ b/solution.py
@@ -16,14 +16,14 @@
     return pltpu.VMEM(dims, dtype)
 
 
-def call(kernel, outs, *operands, from_hbm=0, **static):
+def call(kernel, outs, *operands, from_hbm=0, scratch=(), **static):
     spaces = [pltpu.HBM] * from_hbm + [pltpu.VMEM] * (len(operands) - from_hbm)
     return pl.pallas_call(
         functools.partial(kernel, **static) if static else kernel,
         out_shape=outs,
         in_specs=[pl.BlockSpec(memory_space=space) for space in spaces],
         out_specs=[pl.BlockSpec(memory_space=pltpu.VMEM)] * len(outs),
-        scratch_shapes=[pltpu.SemaphoreType.DMA((from_hbm,))] if from_hbm else [],
+        scratch_shapes=list(scratch),
         compiler_params=pltpu.CompilerParams(vmem_limit_bytes=4 * 2**20),
         name=kernel.__name__,
     )(*[pltpu.with_memory_space_constraint(x, space) for x, space in zip(operands, spaces)])
@@ -67,26 +67,24 @@
 
 
 def head_kernel(*refs):
-    fetched = 4
-    held, (up_ref, down_ref, arrived) = refs[fetched : 2 * fetched], refs[2 * fetched :]
+    fetched = 5
+    held, (pick_ref, up_ref, down_ref, arrived) = refs[fetched : 2 * fetched], refs[2 * fetched :]
     copies = fetch(zip(refs[:fetched], held), arrived)
-    lists_ref, features_ref = held[:2]
+    lists_ref, anchors_ref, features_ref = held[:3]
+    nodes = features_ref.shape[0]
     copies[0].wait()
-    nodes = features_ref.shape[0]
     onehots = [row_counts(lists_ref[0, side : side + 1, :], nodes).astype(BF16) for side in range(2)]
     copies[1].wait()
+    slots = jnp.concatenate([anchors_ref[j : j + 1, :] for j in range(anchors_ref.shape[0])], axis=1)
+    pick_ref[...] = column_counts(slots.T, nodes).astype(BF16)
+    copies[2].wait()
     for onehot, out in zip(onehots, (up_ref, down_ref)):
         out[...] = dot_tn(onehot, features_ref[...]).astype(BF16)
-    for copy in copies[2:]:
+    for copy in copies[3:]:
         copy.wait()
 
 
-def own_kernel(*refs):
-    fetched = 4
-    given, (features_ref, neighbors_ref, anchors_ref) = refs[:fetched], refs[fetched : fetched + 3]
-    held = refs[fetched + 3 : 2 * fetched + 3]
-    own_ref, summed_ref, counts_ref, degree_ref, pick_ref, arrived = refs[2 * fetched + 3 :]
-    copies = fetch(zip(given, held), arrived)
+def own_kernel(features_ref, neighbors_ref, w_self_ref, own_ref, summed_ref, counts_ref, degree_ref):
     features = features_ref[...]
     nodes = features.shape[0]
     edge = counts_ref.shape[1]
@@ -95,12 +93,7 @@
     counts = counts.astype(BF16)
     counts_ref[...] = counts[:, nodes:]
     summed_ref[...] = dot(counts[:, :nodes], features)
-    slots = jnp.concatenate([anchors_ref[j : j + 1, :] for j in range(anchors_ref.shape[0])], axis=1)
-    pick_ref[...] = column_counts(slots.T, nodes).astype(BF16)
-    copies[0].wait()
-    own_ref[...] = dot(features, held[0][...])
-    for copy in copies[1:]:
-        copy.wait()
+    own_ref[...] = dot(features, w_self_ref[...])
 
 
 def embed_kernel(below_ref, above_ref, counts_ref, degree_ref, summed_ref, own_ref, w_neigh_ref, pick_ref, embed_ref, rows_ref):
@@ -160,31 +153,27 @@
     peers, anch = anchors.shape
     slots = peers * anch
     edge = boundary.shape[2]
-    given = (boundary, features, neighbors.T, anchors)
-    _, features, neighbors, anchors, up, down = call(
+    given = (boundary, anchors, features, neighbors.T, w_self)
+    _, anchors, features, neighbors, w_self, pick, up, down = call(
         head_kernel,
-        [shape(x.shape, x.dtype) for x in given] + [shape((edge, width), BF16)] * 2,
+        [shape(x.shape, x.dtype) for x in given] + [shape((slots, nodes), BF16)] + [shape((edge, width), BF16)] * 2,
         *given,
         from_hbm=len(given),
+        scratch=[pltpu.SemaphoreType.DMA((len(given),))],
     )
     below = passed_along(up, "dom", 1)
     above = passed_along(down, "dom", -1)
-    given = (w_self, w_neigh, negatives.transpose(0, 2, 1), positives.T)
-    _, w_neigh, negatives, positives, own, summed, counts, degree, pick = call(
+    own, summed, counts, degree = call(
         own_kernel,
-        [shape(x.shape, x.dtype) for x in given]
-        + [
+        [
             shape((nodes, width), F32),
             shape((nodes, width), F32),
             shape((nodes, 2 * edge), BF16),
             shape((nodes, 1), F32),
-            shape((slots, nodes), BF16),
         ],
-        *given,
         features,
         neighbors,
-        anchors,
-        from_hbm=len(given),
+        w_self,
     )
     embed, rows = call(
         embed_kernel,
@@ -202,8 +191,8 @@
     live, spread, grad = call(
         local_kernel,
         [shape((slots, nodes), BF16), shape((nodes, slots), BF16), shape((nodes, width), F32)],
-        negatives,
-        positives,
+        negatives.transpose(0, 2, 1),
+        positives.T,
         anchors,
         embed,
         scale=scale,
@@ -218,7 +207,7 @@
     )
     terms = exchanged(back, peers)
     [grad] = call(owner_kernel, [shape((nodes, width), F32)], weight, got, grad)
-    [out] = call(final_kernel, [shape((nodes, width), BF16)], spread, terms, grad)
+    [out] = call(final_kernel, [jax.ShapeDtypeStruct((nodes, width), BF16)], spread, terms, grad)
     return (embed, out)
 
 

time: 67.6 us -> 67.5 us (level)
  starting transfers between devices: 24.4 us -> 25.2 us
  waiting for transfers between devices: 31.9 us -> 31.2 us
    all_to_all x2, starting transfers between devices: 11.5 us -> 12.2 us  [exchanged(): lax.all_to_all(block, 'wide', split_axis=0, concat_axis=0, tiled=True)]
    all_to_all x2, waiting for transfers between devices: 31.9 us -> 31.2 us  [exchanged(): lax.all_to_all(block, 'wide', split_axis=0, concat_axis=0, tiled=True)]
    unnamed x2 -> x7, local copies, waits for them, and re-layouts: 1.41 us -> 1.38 us
  transfers between devices with their start and end apart: 4 -> 4, of which waited for: 2 -> 3; matrix products, arithmetic and copies ran while one was open for 1% -> 1% of each run, Pallas kernels for 6% -> 4%
where the time goes in v2:
time: 67.5 us; the launch traced here: 67.1 us
  waiting for transfers between devices  31.2 us (46%)
  starting transfers between devices  25.2 us (37%)
  Pallas kernels  8.51 us (13%)
  local copies, waits for them, and re-layouts  1.38 us (2%)
  between operations  0.72 us (1%)
    all_to_all x2, waiting for transfers between devices, exchanged(): lax.all_to_all(block, 'wide', split_axis=0, concat_axis=0, tiled=True)  31.2 us
    ppermute x2, starting transfers between devices, passed_along(): return lax.ppermute(block, axis, route)  13 us
    all_to_all x2, starting transfers between devices, exchanged(): lax.all_to_all(block, 'wide', split_axis=0, concat_axis=0, tiled=True)  12.2 us
    pallas_call x7, Pallas kernels, call(): pl.pallas_call(functools.partial(kernel, **static) if static else kernel,...  8.51 us
    unnamed x7, local copies, waits for them, and re-layouts  1.38 us
  transfers between devices with their start and end apart: 4, of which 3 were waited for; matrix products, arithmetic and copies ran while one was open for 1% of the time, Pallas kernels for 4%

profile of v2, /device:TPU:7, one launch (start us, length us, event | category | flops | bytes accessed | tf_op | source)
XLA Modules:
  0.0 67.1 jit_solution(11477856345451857539)
XLA Ops:
  0.6 1.9 %head_kernel.1 = (s32[1,2,64]{2,1,0:T(2,128)}, s32[16,32]{1,0:T(8,128)S(1)}, bf16[256,512]{1,0:T(8,128)(2,1)S(1)}, s32[16,256]{1,0:T(8,128)S(1)}, bf16[512,512]{...) custom-call(s32[1,2,64]{2,1,0:T(2,128)} %refs_0_.1, ...), custom_call_target="tpu_custom_call" | custom-call | tf_op jit(solution)/shard_map/head_kernel/pallas_call | solution.py:21
  2.5 0.0 copy-start
  2.5 4.1 %collective-permute-start = (bf16[64,512]{1,0:T(8,128)(2,1)S(1)}, bf16[64,512]{1,0:T(8,128)(2,1)S(1)}, u32[]{:S(2)}, u32[]{:S(2)}) collective-permute-start(bf16[64,512]{1,0:T(8,128)(2,1)S(1)} %get-tuple-element.20), channel_id=1, source_target_pairs={{0,16},{16,32},{32,48},{48,64},{64,80},{80,96},{96,112},{112,128},... | collective-permute-start | bytes 196616 | tf_op jit(solution)/shard_map/ppermute | solution.py:142
  6.7 8.9 %collective-permute-start.1 = (bf16[64,512]{1,0:T(8,128)(2,1)S(1)}, bf16[64,512]{1,0:T(8,128)(2,1)S(1)}, u32[]{:S(2)}, u32[]{:S(2)}) collective-permute-start(bf16[64,512]{1,0:T(8,128)(2,1)S(1)} %get-tuple-element.21), channel_id=1, source_target_pairs={{16,0},{32,16},{48,32},{64,48},{80,64},{96,80},{112,96},{128,112},... | collective-permute-start | bytes 196616 | tf_op jit(solution)/shard_map/ppermute | solution.py:142
  15.5 1.2 %own_kernel.1 = (f32[256,512]{1,0:T(8,128)S(1)}, f32[256,512]{1,0:T(8,128)S(1)}, bf16[256,128]{1,0:T(8,128)(2,1)S(1)}, f32[256,1]{1,0:T(8,128)S(1)}) custom-call(bf16[256,512]{1,0:T(8,128)(2,1)S(1)} %get-tuple-element.22.features_ref, s32[16,256]{1,0:T(8,128)S(1)} %get-tuple-element.23.neighbors_ref, bf16[512,512]{1,0:T(8,128)(2,1)S(1)} %get-tuple-element.24.w_self_ref), custom_call_target="tpu_custom_call" | custom-call | tf_op jit(solution)/shard_map/own_kernel/pallas_call | solution.py:21
  16.8 0.0 collective-permute-done.below_ref
  16.8 0.1 collective-permute-done.1.above_ref
  16.8 0.0 copy-done
  16.8 1.6 %embed_kernel.1 = (bf16[256,512]{1,0:T(8,128)(2,1)S(1)}, bf16[512,512]{1,0:T(8,128)(2,1)}) custom-call(bf16[64,512]{1,0:T(8,128)(2,1)S(1)} %collective-permute-done.below_ref, bf16[64,512]{1,0:T(8,128)(2,1)S(1)} %collective-permute-done.1.above_ref, bf16[256,128]{1,0:T(8,128)(2,1)S(1)} %get-tuple-element.25.counts_ref, ...), custom_call_target="tpu_custom_call" | custom-call | tf_op jit(solution)/shard_map/embed_kernel/pallas_call | solution.py:21
  18.4 0.0 copy-start.1
  18.4 8.8 %all-to-all-start = ((bf16[16,32,512]{2,1,0:T(8,128)(2,1)}), bf16[16,32,512]{2,1,0:T(8,128)(2,1)S(1)}, u32[]{:S(2)}, u32[]{:S(2)}) async-start(bf16[16,32,512]{2,1,0:T(8,128)(2,1)} %bitcast.3), calls=%async_computation | async-start | bytes 1048576 | tf_op jit(solution)/shard_map/all_to_all | solution.py:147
  27.2 0.0 copy-start.2
  27.2 0.0 copy-done.1
  27.2 0.7 copy-done.2
  27.9 1.0 %local_kernel.1 = (bf16[512,256]{1,0:T(8,128)(2,1)S(1)}, bf16[256,512]{1,0:T(8,128)(2,1)S(1)}, f32[256,512]{1,0:T(8,128)S(1)}) custom-call(s32[16,8,32]{2,1,0:T(8,128)S(1)} %bitcast.10, s32[2,256]{1,0:T(2,128)S(1)} %bitcast.11, s32[16,32]{1,0:T(8,128)S(1)} %get-tuple-element.31.anchors_ref, bf16[256,512]{1,0:T(8,128)(2,1)S(1)} %get-tuple-element.38.embed_ref), custom_call_target="tpu_custom_call" | custom-call | tf_op jit(solution)/shard_map/local_kernel/pallas_call | solution.py:21
  28.9 15.5 %all-to-all-done = bf16[16,32,512]{2,1,0:T(8,128)(2,1)S(1)} async-done(((bf16[16,32,512]{2,1,0:T(8,128)(2,1)}), bf16[16,32,512]{2,1,0:T(8,128)(2,1)S(1)}, u32[]{:S(2)}, u32[]{:S(2)}) %all-to-all-start) | async-done | bytes 524320 | tf_op jit(solution)/shard_map/all_to_all | solution.py:147
  44.4 1.5 %score_kernel.1 = (bf16[512,256]{1,0:T(8,128)(2,1)S(1)}, bf16[512,512]{1,0:T(8,128)(2,1)}) custom-call(bf16[512,512]{1,0:T(8,128)(2,1)S(1)} %bitcast.7, bf16[256,512]{1,0:T(8,128)(2,1)S(1)} %get-tuple-element.38.embed_ref, bf16[512,256]{1,0:T(8,128)(2,1)S(1)} %get-tuple-element.34.live_ref), custom_call_target="tpu_custom_call" | custom-call | tf_op jit(solution)/shard_map/score_kernel/pallas_call | solution.py:21
  45.9 3.5 %all-to-all-start.1 = ((bf16[16,32,512]{2,1,0:T(8,128)(2,1)}), bf16[16,32,512]{2,1,0:T(8,128)(2,1)S(1)}, u32[]{:S(2)}, u32[]{:S(2)}) async-start(bf16[16,32,512]{2,1,0:T(8,128)(2,1)} %bitcast.5), calls=%async_computation.1 | async-start | bytes 1048576 | tf_op jit(solution)/shard_map/all_to_all | solution.py:147
  49.4 0.7 %copy.10 = bf16[256,512]{1,0:T(8,128)(2,1)} copy(bf16[256,512]{1,0:T(8,128)(2,1)S(1)} %get-tuple-element.38.embed_ref) | data formatting | bytes 524288
  50.1 0.3 owner_kernel.1.grad_ref
  50.4 15.7 %all-to-all-done.1 = bf16[16,32,512]{2,1,0:T(8,128)(2,1)S(1)} async-done(((bf16[16,32,512]{2,1,0:T(8,128)(2,1)}), bf16[16,32,512]{2,1,0:T(8,128)(2,1)S(1)}, u32[]{:S(2)}, u32[]{:S(2)}) %all-to-all-start.1) | async-done | bytes 524320 | tf_op jit(solution)/shard_map/all_to_all | solution.py:147
  66.1 1.0 %final_kernel.1 = bf16[256,512]{1,0:T(8,128)(2,1)} custom-call(bf16[256,512]{1,0:T(8,128)(2,1)S(1)} %get-tuple-element.32.spread_ref, bf16[512,512]{1,0:T(8,128)(2,1)S(1)} %bitcast.9, f32[256,512]{1,0:T(8,128)S(1)} %owner_kernel.1.grad_ref), custom_call_target="tpu_custom_call" | custom-call | tf_op jit(solution)/shard_map/final_kernel/pallas_call | solution.py:21
Async XLA Ops:
  2.5 14.3 %copy-start = (bf16[512,512]{1,0:T(8,128)(2,1)S(1)}, bf16[512,512]{1,0:T(8,128)(2,1)}, u32[]{:S(2)}) copy-start(bf16[512,512]{1,0:T(8,128)(2,1)} %w_neigh_ref.1) | copy-start | bytes 1572868
  2.5 14.3 %collective-permute-start = (bf16[64,512]{1,0:T(8,128)(2,1)S(1)}, bf16[64,512]{1,0:T(8,128)(2,1)S(1)}, u32[]{:S(2)}, u32[]{:S(2)}) collective-permute-start(bf16[64,512]{1,0:T(8,128)(2,1)S(1)} %get-tuple-element.20), channel_id=1, source_target_pairs={{0,16},{16,32},{32,48},{48,64},{64,80},{80,96},{96,112},{112,128},... | collective-permute-start | bytes 196616 | tf_op jit(solution)/shard_map/ppermute | solution.py:142
  6.7 10.2 %collective-permute-start.1 = (bf16[64,512]{1,0:T(8,128)(2,1)S(1)}, bf16[64,512]{1,0:T(8,128)(2,1)S(1)}, u32[]{:S(2)}, u32[]{:S(2)}) collective-permute-start(bf16[64,512]{1,0:T(8,128)(2,1)S(1)} %get-tuple-element.21), channel_id=1, source_target_pairs={{16,0},{32,16},{48,32},{64,48},{80,64},{96,80},{112,96},{128,112},... | collective-permute-start | bytes 196616 | tf_op jit(solution)/shard_map/ppermute | solution.py:142
  18.4 8.8 %copy-start.1 = (s32[16,32,8]{1,2,0:T(8,128)S(1)}, s32[16,32,8]{1,2,0:T(8,128)}, u32[]{:S(2)}) copy-start(s32[16,32,8]{1,2,0:T(8,128)} %param.14) | copy-start | bytes 49156
  18.4 26.0 %all-to-all-start = ((bf16[16,32,512]{2,1,0:T(8,128)(2,1)}), bf16[16,32,512]{2,1,0:T(8,128)(2,1)S(1)}, u32[]{:S(2)}, u32[]{:S(2)}) async-start(bf16[16,32,512]{2,1,0:T(8,128)(2,1)} %bitcast.3), calls=%async_computation | async-start | bytes 1048576 | tf_op jit(solution)/shard_map/all_to_all | solution.py:147
  27.2 0.7 %copy-start.2 = (s32[256,2]{0,1:T(2,128)S(1)}, s32[256,2]{0,1:T(2,128)}, u32[]{:S(2)}) copy-start(s32[256,2]{0,1:T(2,128)} %param.15) | copy-start | bytes 6148
  45.9 20.2 %all-to-all-start.1 = ((bf16[16,32,512]{2,1,0:T(8,128)(2,1)}), bf16[16,32,512]{2,1,0:T(8,128)(2,1)S(1)}, u32[]{:S(2)}, u32[]{:S(2)}) async-start(bf16[16,32,512]{2,1,0:T(8,128)(2,1)} %bitcast.5), calls=%async_computation.1 | async-start | bytes 1048576 | tf_op jit(solution)/shard_map/all_to_all | solution.py:147

commit v3 on v2

--- a/solution.py
+++ b/solution.py
@@ -48,12 +48,14 @@
     return lax.dot_general(a, b, (((0,), (0,)), ((), ())), preferred_element_type=F32)
 
 
-def column_counts(columns, width, offset=0):
+def column_counts(columns, width):
     rows, slots = columns.shape
-    lanes = lax.broadcasted_iota(jnp.int32, (rows, width), 1) + offset
-    total = jnp.zeros((rows, width), F32)
+    lanes = (lax.broadcasted_iota(jnp.int32, (rows, width), 1) - 128).astype(BF16)
+    columns = (columns - 128).astype(BF16)
+    total = jnp.zeros((rows, width), BF16)
+    one, zero = jnp.ones((), BF16), jnp.zeros((), BF16)
     for slot in range(slots):
-        total = total + jnp.where(columns[:, slot : slot + 1] == lanes, 1.0, 0.0)
+        total = total + jnp.where(columns[:, slot : slot + 1] == lanes, one, zero)
     return total
 
 
@@ -67,7 +69,7 @@
 
 
 def head_kernel(*refs):
-    fetched = 5
+    fetched = 4
     held, (pick_ref, up_ref, down_ref, arrived) = refs[fetched : 2 * fetched], refs[2 * fetched :]
     copies = fetch(zip(refs[:fetched], held), arrived)
     lists_ref, anchors_ref, features_ref = held[:3]
@@ -76,7 +78,7 @@
     onehots = [row_counts(lists_ref[0, side : side + 1, :], nodes).astype(BF16) for side in range(2)]
     copies[1].wait()
     slots = jnp.concatenate([anchors_ref[j : j + 1, :] for j in range(anchors_ref.shape[0])], axis=1)
-    pick_ref[...] = column_counts(slots.T, nodes).astype(BF16)
+    pick_ref[...] = column_counts(slots.T, nodes)
     copies[2].wait()
     for onehot, out in zip(onehots, (up_ref, down_ref)):
         out[...] = dot_tn(onehot, features_ref[...]).astype(BF16)
@@ -84,15 +86,16 @@
         copy.wait()
 
 
-def own_kernel(features_ref, neighbors_ref, w_self_ref, own_ref, summed_ref, counts_ref, degree_ref):
+def own_kernel(w_self_hbm, features_ref, neighbors_ref, own_ref, summed_ref, counts_ref, degree_ref, w_self_ref, arrived):
+    [copy] = fetch(((w_self_hbm, w_self_ref),), arrived)
     features = features_ref[...]
     nodes = features.shape[0]
     edge = counts_ref.shape[1]
     counts = column_counts(neighbors_ref[...].T, nodes + edge)
-    degree_ref[...] = jnp.sum(counts, axis=1, keepdims=True)
-    counts = counts.astype(BF16)
+    degree_ref[...] = jnp.sum(counts.astype(F32), axis=1, keepdims=True)
     counts_ref[...] = counts[:, nodes:]
     summed_ref[...] = dot(counts[:, :nodes], features)
+    copy.wait()
     own_ref[...] = dot(features, w_self_ref[...])
 
 
@@ -105,12 +108,13 @@
     rows_ref[...] = dot(pick_ref[...], embed).astype(BF16)
 
 
-def local_kernel(negatives_ref, positives_ref, anchors_ref, embed_ref, live_ref, spread_ref, grad_ref, *, scale):
+def local_kernel(negatives_ref, positives_ref, anchors_ref, embed_ref, out_ref, live_ref, spread_ref, grad_ref, *, scale):
     embed = embed_ref[...]
+    out_ref[...] = embed
     nodes = embed.shape[0]
     peers = negatives_ref.shape[0]
     slots = jnp.concatenate([negatives_ref[j] for j in range(peers)], axis=1)
-    live_ref[...] = column_counts(slots.T, nodes).astype(BF16)
+    live_ref[...] = column_counts(slots.T, nodes)
     anchors = jnp.concatenate([anchors_ref[j : j + 1, :] for j in range(peers)], axis=1)
     spread_ref[...] = row_counts(anchors, nodes).astype(BF16)
     first = row_counts(positives_ref[0:1, :], nodes).astype(BF16)
@@ -128,12 +132,9 @@
     back_ref[...] = dot(weight, embed).astype(BF16)
 
 
-def owner_kernel(weight_ref, got_ref, grad_ref, out_ref):
-    out_ref[...] = grad_ref[...] + dot_tn(weight_ref[...], got_ref[...])
-
-
-def final_kernel(spread_ref, terms_ref, grad_ref, out_ref):
-    out_ref[...] = (grad_ref[...] + dot(spread_ref[...], terms_ref[...])).astype(BF16)
+def final_kernel(spread_ref, terms_ref, weight_ref, got_ref, grad_ref, out_ref):
+    total = grad_ref[...] + dot_tn(weight_ref[...], got_ref[...]) + dot(spread_ref[...], terms_ref[...])
+    out_ref[...] = total.astype(BF16)
 
 
 def passed_along(block, axis, distance):
@@ -153,8 +154,8 @@
     peers, anch = anchors.shape
     slots = peers * anch
     edge = boundary.shape[2]
-    given = (boundary, anchors, features, neighbors.T, w_self)
-    _, anchors, features, neighbors, w_self, pick, up, down = call(
+    given = (boundary, anchors, features, neighbors.T)
+    _, anchors, features, neighbors, pick, up, down = call(
         head_kernel,
         [shape(x.shape, x.dtype) for x in given] + [shape((slots, nodes), BF16)] + [shape((edge, width), BF16)] * 2,
         *given,
@@ -171,9 +172,11 @@
             shape((nodes, 2 * edge), BF16),
             shape((nodes, 1), F32),
         ],
+        w_self,
         features,
         neighbors,
-        w_self,
+        from_hbm=1,
+        scratch=[pltpu.VMEM(w_self.shape, BF16), pltpu.SemaphoreType.DMA((1,))],
     )
     embed, rows = call(
         embed_kernel,
@@ -188,9 +191,9 @@
         pick,
     )
     got = exchanged(rows, peers)
-    live, spread, grad = call(
+    embedded, live, spread, grad = call(
         local_kernel,
-        [shape((slots, nodes), BF16), shape((nodes, slots), BF16), shape((nodes, width), F32)],
+        [jax.ShapeDtypeStruct((nodes, width), BF16), shape((slots, nodes), BF16), shape((nodes, slots), BF16), shape((nodes, width), F32)],
         negatives.transpose(0, 2, 1),
         positives.T,
         anchors,
@@ -206,9 +209,8 @@
         scale=scale,
     )
     terms = exchanged(back, peers)
-    [grad] = call(owner_kernel, [shape((nodes, width), F32)], weight, got, grad)
-    [out] = call(final_kernel, [jax.ShapeDtypeStruct((nodes, width), BF16)], spread, terms, grad)
-    return (embed, out)
+    [out] = call(final_kernel, [jax.ShapeDtypeStruct((nodes, width), BF16)], spread, terms, weight, got, grad)
+    return (embedded, out)
 
 
 def solution(mesh):

time: 67.5 us -> 66.5 us (0.985)
  blocking collectives: 0 us -> 20 us
  waiting for transfers between devices: 31.2 us -> 15.7 us
  starting transfers between devices: 25.2 us -> 21.5 us
  Pallas kernels: 8.51 us -> 7.5 us
  local copies, waits for them, and re-layouts: 1.38 us -> 0.67 us
    all_to_all x0 -> x1, blocking collectives: none -> 20 us  [exchanged(): lax.all_to_all(block, 'wide', split_axis=0, concat_axis=0, tiled=True)]
    all_to_all x2 -> x1, waiting for transfers between devices: 31.2 us -> 15.7 us  [exchanged(): lax.all_to_all(block, 'wide', split_axis=0, concat_axis=0, tiled=True)]
    all_to_all x2 -> x1, starting transfers between devices: 12.2 us -> 8.69 us  [exchanged(): lax.all_to_all(block, 'wide', split_axis=0, concat_axis=0, tiled=True)]
    pallas_call x7 -> x6, Pallas kernels: 8.51 us -> 7.5 us  [call(): pl.pallas_call(functools.partial(kernel, **static) if static else kernel,...]
    unnamed x7 -> x6, local copies, waits for them, and re-layouts: 1.38 us -> 0.67 us
  transfers between devices with their start and end apart: 4 -> 3, of which waited for: 3 -> 1; matrix products, arithmetic and copies ran while one was open for 1% -> 0% of each run, Pallas kernels for 4% -> 3%
where the time goes in v3:
time: 66.5 us; the launch traced here: 66.1 us
  starting transfers between devices  21.5 us (32%)
  blocking collectives  20 us (30%)
  waiting for transfers between devices  15.7 us (24%)
  Pallas kernels  7.5 us (11%)
  between operations  0.72 us (1%)
  local copies, waits for them, and re-layouts  0.67 us (1%)
    all_to_all x1, blocking collectives, exchanged(): lax.all_to_all(block, 'wide', split_axis=0, concat_axis=0, tiled=True)  20 us
    all_to_all x1, waiting for transfers between devices, exchanged(): lax.all_to_all(block, 'wide', split_axis=0, concat_axis=0, tiled=True)  15.7 us
    ppermute x2, starting transfers between devices, passed_along(): return lax.ppermute(block, axis, route)  12.9 us
    all_to_all x1, starting transfers between devices, exchanged(): lax.all_to_all(block, 'wide', split_axis=0, concat_axis=0, tiled=True)  8.69 us
    pallas_call x6, Pallas kernels, call(): pl.pallas_call(functools.partial(kernel, **static) if static else kernel,...  7.5 us
  transfers between devices with their start and end apart: 3, of which 1 were waited for; matrix products, arithmetic and copies ran while one was open for 0% of the time, Pallas kernels for 3%

profile of v3, /device:TPU:7, one launch (start us, length us, event | category | flops | bytes accessed | tf_op | source)
XLA Modules:
  0.0 66.1 jit_solution(18406335273100593596)
XLA Ops:
  0.6 0.0 copy-start
  0.6 1.9 %head_kernel.1 = (s32[1,2,64]{2,1,0:T(2,128)}, s32[16,32]{1,0:T(8,128)S(1)}, bf16[256,512]{1,0:T(8,128)(2,1)S(1)}, s32[16,256]{1,0:T(8,128)S(1)}, bf16[512,256]{...) custom-call(s32[1,2,64]{2,1,0:T(2,128)} %refs_0_.1, s32[16,32]{1,0:T(8,128)} %refs_1_.1, ...), custom_call_target="tpu_custom_call" | custom-call | tf_op jit(solution)/shard_map/head_kernel/pallas_call | solution.py:21
  2.6 4.0 %collective-permute-start = (bf16[64,512]{1,0:T(8,128)(2,1)S(1)}, bf16[64,512]{1,0:T(8,128)(2,1)S(1)}, u32[]{:S(2)}, u32[]{:S(2)}) collective-permute-start(bf16[64,512]{1,0:T(8,128)(2,1)S(1)} %get-tuple-element.21), channel_id=1, source_target_pairs={{0,16},{16,32},{32,48},{48,64},{64,80},{80,96},{96,112},{112,128},... | collective-permute-start | bytes 196616 | tf_op jit(solution)/shard_map/ppermute | solution.py:143
  6.6 8.9 %collective-permute-start.1 = (bf16[64,512]{1,0:T(8,128)(2,1)S(1)}, bf16[64,512]{1,0:T(8,128)(2,1)S(1)}, u32[]{:S(2)}, u32[]{:S(2)}) collective-permute-start(bf16[64,512]{1,0:T(8,128)(2,1)S(1)} %get-tuple-element.22), channel_id=1, source_target_pairs={{16,0},{32,16},{48,32},{64,48},{80,64},{96,80},{112,96},{128,112},... | collective-permute-start | bytes 196616 | tf_op jit(solution)/shard_map/ppermute | solution.py:143
  15.4 1.4 %own_kernel.1 = (f32[256,512]{1,0:T(8,128)S(1)}, f32[256,512]{1,0:T(8,128)S(1)}, bf16[256,128]{1,0:T(8,128)(2,1)S(1)}, f32[256,1]{1,0:T(8,128)S(1)}) custom-call(bf16[512,512]{1,0:T(8,128)(2,1)} %w_self_hbm.1, bf16[256,512]{1,0:T(8,128)(2,1)S(1)} %get-tuple-element.23.features_ref, s32[16,256]{1,0:T(8,128)S(1)} %get-tuple-element.24.neighbors_ref), custom_call_target="tpu_custom_call" | custom-call | tf_op jit(solution)/shard_map/own_kernel/pallas_call | solution.py:21
  16.8 0.0 collective-permute-done.below_ref
  16.8 0.0 collective-permute-done.1.above_ref
  16.8 0.0 copy-done
  16.8 1.5 %embed_kernel.1 = (bf16[256,512]{1,0:T(8,128)(2,1)S(1)}, bf16[512,512]{1,0:T(8,128)(2,1)}) custom-call(bf16[64,512]{1,0:T(8,128)(2,1)S(1)} %collective-permute-done.below_ref, bf16[64,512]{1,0:T(8,128)(2,1)S(1)} %collective-permute-done.1.above_ref, bf16[256,128]{1,0:T(8,128)(2,1)S(1)} %get-tuple-element.25.counts_ref, ...), custom_call_target="tpu_custom_call" | custom-call | tf_op jit(solution)/shard_map/embed_kernel/pallas_call | solution.py:21
  18.4 0.0 copy-start.1
  18.4 8.7 %all-to-all-start = ((bf16[16,32,512]{2,1,0:T(8,128)(2,1)}), bf16[16,32,512]{2,1,0:T(8,128)(2,1)S(1)}, u32[]{:S(2)}, u32[]{:S(2)}) async-start(bf16[16,32,512]{2,1,0:T(8,128)(2,1)} %bitcast.3), calls=%async_computation | async-start | bytes 1048576 | tf_op jit(solution)/shard_map/all_to_all | solution.py:148
  27.1 0.0 copy-start.2
  27.1 0.0 copy-done.1
  27.1 0.7 %copy-done.2 = s32[256,2]{0,1:T(2,128)S(1)} copy-done((s32[256,2]{0,1:T(2,128)S(1)}, s32[256,2]{0,1:T(2,128)}, u32[]{:S(2)}) %copy-start.2) | copy-done | bytes 2072
  27.7 0.8 %local_kernel.1 = (bf16[256,512]{1,0:T(8,128)(2,1)}, bf16[512,256]{1,0:T(8,128)(2,1)S(1)}, bf16[256,512]{1,0:T(8,128)(2,1)S(1)}, f32[256,512]{1,0:T(8,128)S(1)}) custom-call(s32[16,8,32]{2,1,0:T(8,128)S(1)} %bitcast.11, s32[2,256]{1,0:T(2,128)S(1)} %bitcast.12, s32[16,32]{1,0:T(8,128)S(1)} %get-tuple-element.20.anchors_ref, ...), custom_call_target="tpu_custom_call" | custom-call | tf_op jit(solution)/shard_map/local_kernel/pallas_call | solution.py:21
  28.5 15.7 %all-to-all-done = bf16[16,32,512]{2,1,0:T(8,128)(2,1)S(1)} async-done(((bf16[16,32,512]{2,1,0:T(8,128)(2,1)}), bf16[16,32,512]{2,1,0:T(8,128)(2,1)S(1)}, u32[]{:S(2)}, u32[]{:S(2)}) %all-to-all-start) | async-done | bytes 524320 | tf_op jit(solution)/shard_map/all_to_all | solution.py:148
  44.3 0.7 %score_kernel.1 = (bf16[512,256]{1,0:T(8,128)(2,1)S(1)}, bf16[512,512]{1,0:T(8,128)(2,1)S(1)}) custom-call(bf16[512,512]{1,0:T(8,128)(2,1)S(1)} %bitcast.7, bf16[256,512]{1,0:T(8,128)(2,1)S(1)} %get-tuple-element.30.embed_ref, bf16[512,256]{1,0:T(8,128)(2,1)S(1)} %get-tuple-element.34.live_ref), custom_call_target="tpu_custom_call" | custom-call | tf_op jit(solution)/shard_map/score_kernel/pallas_call | solution.py:21
  45.0 20.0 %all_to_all.10 = bf16[16,32,512]{2,1,0:T(8,128)(2,1)S(1)} all-to-all(bf16[16,32,512]{2,1,0:T(8,128)(2,1)S(1)} %bitcast.10), channel_id=1, replica_groups=mesh['dom'=32,'wide'=16] {'wide'}, dimensions={0} | all-to-all | bytes 1048576 | tf_op jit(solution)/shard_map/all_to_all | solution.py:148
  65.0 1.2 %final_kernel.1 = bf16[256,512]{1,0:T(8,128)(2,1)} custom-call(bf16[256,512]{1,0:T(8,128)(2,1)S(1)} %get-tuple-element.32.spread_ref, bf16[512,512]{1,0:T(8,128)(2,1)S(1)} %bitcast.9, bf16[512,256]{1,0:T(8,128)(2,1)S(1)} %get-tuple-element.36.weight_ref, bf16[512,512]{1,0:T(8,128)(2,1)S(1)} %bitcast.8, f32[256,512]{1,0:T(8,128)S(1)} %get-tuple-element.37.grad_ref), custom_call_target="tpu_custom_call" | custom-call | tf_op jit(solution)/shard_map/final_kernel/pallas_call | solution.py:21
Async XLA Ops:
  0.6 16.2 %copy-start = (bf16[512,512]{1,0:T(8,128)(2,1)S(1)}, bf16[512,512]{1,0:T(8,128)(2,1)}, u32[]{:S(2)}) copy-start(bf16[512,512]{1,0:T(8,128)(2,1)} %w_neigh_ref.1) | copy-start | bytes 1572868
  2.6 14.2 %collective-permute-start = (bf16[64,512]{1,0:T(8,128)(2,1)S(1)}, bf16[64,512]{1,0:T(8,128)(2,1)S(1)}, u32[]{:S(2)}, u32[]{:S(2)}) collective-permute-start(bf16[64,512]{1,0:T(8,128)(2,1)S(1)} %get-tuple-element.21), channel_id=1, source_target_pairs={{0,16},{16,32},{32,48},{48,64},{64,80},{80,96},{96,112},{112,128},... | collective-permute-start | bytes 196616 | tf_op jit(solution)/shard_map/ppermute | solution.py:143
  6.6 10.2 %collective-permute-start.1 = (bf16[64,512]{1,0:T(8,128)(2,1)S(1)}, bf16[64,512]{1,0:T(8,128)(2,1)S(1)}, u32[]{:S(2)}, u32[]{:S(2)}) collective-permute-start(bf16[64,512]{1,0:T(8,128)(2,1)S(1)} %get-tuple-element.22), channel_id=1, source_target_pairs={{16,0},{32,16},{48,32},{64,48},{80,64},{96,80},{112,96},{128,112},... | collective-permute-start | bytes 196616 | tf_op jit(solution)/shard_map/ppermute | solution.py:143
  18.4 8.7 %copy-start.1 = (s32[16,32,8]{1,2,0:T(8,128)S(1)}, s32[16,32,8]{1,2,0:T(8,128)}, u32[]{:S(2)}) copy-start(s32[16,32,8]{1,2,0:T(8,128)} %param.14) | copy-start | bytes 49156
  18.4 25.9 %all-to-all-start = ((bf16[16,32,512]{2,1,0:T(8,128)(2,1)}), bf16[16,32,512]{2,1,0:T(8,128)(2,1)S(1)}, u32[]{:S(2)}, u32[]{:S(2)}) async-start(bf16[16,32,512]{2,1,0:T(8,128)(2,1)} %bitcast.3), calls=%async_computation | async-start | bytes 1048576 | tf_op jit(solution)/shard_map/all_to_all | solution.py:148
  27.1 0.7 %copy-start.2 = (s32[256,2]{0,1:T(2,128)S(1)}, s32[256,2]{0,1:T(2,128)}, u32[]{:S(2)}) copy-start(s32[256,2]{0,1:T(2,128)} %param.15) | copy-start | bytes 6148

commit v4 on v3

--- a/solution.py
+++ b/solution.py
@@ -16,14 +16,16 @@
     return pltpu.VMEM(dims, dtype)
 
 
-def call(kernel, outs, *operands, from_hbm=0, scratch=(), **static):
+def call(kernel, outs, *operands, from_hbm=0, scratch=(), aliases=None, **static):
     spaces = [pltpu.HBM] * from_hbm + [pltpu.VMEM] * (len(operands) - from_hbm)
+    out_spaces = [pltpu.HBM if isinstance(x, jax.ShapeDtypeStruct) else pltpu.VMEM for x in outs]
     return pl.pallas_call(
         functools.partial(kernel, **static) if static else kernel,
         out_shape=outs,
         in_specs=[pl.BlockSpec(memory_space=space) for space in spaces],
-        out_specs=[pl.BlockSpec(memory_space=pltpu.VMEM)] * len(outs),
+        out_specs=[pl.BlockSpec(memory_space=space) for space in out_spaces],
         scratch_shapes=list(scratch),
+        input_output_aliases=aliases or {},
         compiler_params=pltpu.CompilerParams(vmem_limit_bytes=4 * 2**20),
         name=kernel.__name__,
     )(*[pltpu.with_memory_space_constraint(x, space) for x, space in zip(operands, spaces)])
@@ -69,7 +71,7 @@
 
 
 def head_kernel(*refs):
-    fetched = 4
+    fetched = 5
     held, (pick_ref, up_ref, down_ref, arrived) = refs[fetched : 2 * fetched], refs[2 * fetched :]
     copies = fetch(zip(refs[:fetched], held), arrived)
     lists_ref, anchors_ref, features_ref = held[:3]
@@ -86,17 +88,31 @@
         copy.wait()
 
 
-def own_kernel(w_self_hbm, features_ref, neighbors_ref, own_ref, summed_ref, counts_ref, degree_ref, w_self_ref, arrived):
-    [copy] = fetch(((w_self_hbm, w_self_ref),), arrived)
-    features = features_ref[...]
-    nodes = features.shape[0]
-    edge = counts_ref.shape[1]
-    counts = column_counts(neighbors_ref[...].T, nodes + edge)
-    degree_ref[...] = jnp.sum(counts.astype(F32), axis=1, keepdims=True)
-    counts_ref[...] = counts[:, nodes:]
-    summed_ref[...] = dot(counts[:, :nodes], features)
-    copy.wait()
-    own_ref[...] = dot(features, w_self_ref[...])
+def own_kernel(*refs, turn, made):
+    w_self_hbm, features_ref, neighbors_ref, negatives_ref, positives_ref, anchors_ref = refs[:6]
+    own_ref, summed_ref, counts_ref, degree_ref, live_ref, spread_ref, pairs_ref = refs[len(refs) - made - 2 : -2]
+    w_self_ref, arrived = refs[-2:]
+
+    @pl.when(waits_long() if turn == 0 else jnp.logical_not(waits_long()))
+    def _():
+        [copy] = fetch(((w_self_hbm, w_self_ref),), arrived)
+        features = features_ref[...]
+        nodes = features.shape[0]
+        edge = counts_ref.shape[1]
+        peers = negatives_ref.shape[0]
+        counts = column_counts(neighbors_ref[...].T, nodes + edge)
+        degree_ref[...] = jnp.sum(counts.astype(F32), axis=1, keepdims=True)
+        counts_ref[...] = counts[:, nodes:]
+        summed_ref[...] = dot(counts[:, :nodes], features)
+        slots = jnp.concatenate([negatives_ref[j] for j in range(peers)], axis=1)
+        live_ref[...] = column_counts(slots.T, nodes)
+        anchors = jnp.concatenate([anchors_ref[j : j + 1, :] for j in range(peers)], axis=1)
+        spread_ref[...] = row_counts(anchors, nodes).astype(BF16)
+        first = row_counts(positives_ref[0:1, :], nodes).astype(BF16)
+        second = row_counts(positives_ref[1:2, :], nodes).astype(BF16)
+        pairs_ref[...] = dot_nt(first, second) + dot_nt(second, first)
+        copy.wait()
+        own_ref[...] = dot(features, w_self_ref[...])
 
 
 def embed_kernel(below_ref, above_ref, counts_ref, degree_ref, summed_ref, own_ref, w_neigh_ref, pick_ref, embed_ref, rows_ref):
@@ -108,33 +124,29 @@
     rows_ref[...] = dot(pick_ref[...], embed).astype(BF16)
 
 
-def local_kernel(negatives_ref, positives_ref, anchors_ref, embed_ref, out_ref, live_ref, spread_ref, grad_ref, *, scale):
-    embed = embed_ref[...]
-    out_ref[...] = embed
-    nodes = embed.shape[0]
-    peers = negatives_ref.shape[0]
-    slots = jnp.concatenate([negatives_ref[j] for j in range(peers)], axis=1)
-    live_ref[...] = column_counts(slots.T, nodes)
-    anchors = jnp.concatenate([anchors_ref[j : j + 1, :] for j in range(peers)], axis=1)
-    spread_ref[...] = row_counts(anchors, nodes).astype(BF16)
-    first = row_counts(positives_ref[0:1, :], nodes).astype(BF16)
-    second = row_counts(positives_ref[1:2, :], nodes).astype(BF16)
-    pairs = dot_nt(first, second) + dot_nt(second, first)
-    weight = (jax.nn.sigmoid(dot_nt(embed, embed) * scale) - 1.0) * pairs
-    grad_ref[...] = dot(weight.astype(BF16), embed)
-
-
-def score_kernel(got_ref, embed_ref, live_ref, weight_ref, back_ref, *, scale):
+def score_kernel(got_ref, embed_ref, live_ref, pairs_ref, weight_ref, back_ref, grad_ref, out_ref, sent, *, scale):
+    copy = pltpu.make_async_copy(embed_ref, out_ref, sent.at[0])
+    copy.start()
     embed = embed_ref[...]
     weight = jax.nn.sigmoid(dot_nt(got_ref[...], embed) * scale) * live_ref[...].astype(F32)
     weight = weight.astype(BF16)
     weight_ref[...] = weight
     back_ref[...] = dot(weight, embed).astype(BF16)
+    weight = (jax.nn.sigmoid(dot_nt(embed, embed) * scale) - 1.0) * pairs_ref[...]
+    grad_ref[...] = dot(weight.astype(BF16), embed)
+    copy.wait()
 
 
 def final_kernel(spread_ref, terms_ref, weight_ref, got_ref, grad_ref, out_ref):
     total = grad_ref[...] + dot_tn(weight_ref[...], got_ref[...]) + dot(spread_ref[...], terms_ref[...])
     out_ref[...] = total.astype(BF16)
+
+
+ROW = 8
+
+
+def waits_long():
+    return lax.rem(lax.axis_index("dom"), ROW) == 0
 
 
 def passed_along(block, axis, distance):
@@ -154,29 +166,32 @@
     peers, anch = anchors.shape
     slots = peers * anch
     edge = boundary.shape[2]
-    given = (boundary, anchors, features, neighbors.T)
-    _, anchors, features, neighbors, pick, up, down = call(
+    given = (boundary, anchors, features, neighbors.T, positives.T)
+    _, anchors, features, neighbors, positives, pick, up, down = call(
         head_kernel,
         [shape(x.shape, x.dtype) for x in given] + [shape((slots, nodes), BF16)] + [shape((edge, width), BF16)] * 2,
         *given,
         from_hbm=len(given),
         scratch=[pltpu.SemaphoreType.DMA((len(given),))],
     )
+    local = (w_self, features, neighbors, negatives.transpose(0, 2, 1), positives, anchors)
+    made = [
+        shape((nodes, width), F32),
+        shape((nodes, width), F32),
+        shape((nodes, 2 * edge), BF16),
+        shape((nodes, 1), F32),
+        shape((slots, nodes), BF16),
+        shape((nodes, slots), BF16),
+        shape((nodes, nodes), F32),
+    ]
     below = passed_along(up, "dom", 1)
+    room = [pltpu.VMEM(w_self.shape, BF16), pltpu.SemaphoreType.DMA((1,))]
+    early = call(own_kernel, made, *local, from_hbm=1, scratch=room, turn=0, made=len(made))
+    down, early = lax.optimization_barrier((down, early))
     above = passed_along(down, "dom", -1)
-    own, summed, counts, degree = call(
-        own_kernel,
-        [
-            shape((nodes, width), F32),
-            shape((nodes, width), F32),
-            shape((nodes, 2 * edge), BF16),
-            shape((nodes, 1), F32),
-        ],
-        w_self,
-        features,
-        neighbors,
-        from_hbm=1,
-        scratch=[pltpu.VMEM(w_self.shape, BF16), pltpu.SemaphoreType.DMA((1,))],
+    aliases = {len(local) + n: n for n in range(len(made))}
+    own, summed, counts, degree, live, spread, pairs = call(
+        own_kernel, made, *local, *early, from_hbm=1, scratch=room, aliases=aliases, turn=1, made=len(made)
     )
     embed, rows = call(
         embed_kernel,
@@ -191,25 +206,23 @@
         pick,
     )
     got = exchanged(rows, peers)
-    embedded, live, spread, grad = call(
-        local_kernel,
-        [jax.ShapeDtypeStruct((nodes, width), BF16), shape((slots, nodes), BF16), shape((nodes, slots), BF16), shape((nodes, width), F32)],
-        negatives.transpose(0, 2, 1),
-        positives.T,
-        anchors,
-        embed,
-        scale=scale,
-    )
-    weight, back = call(
+    weight, back, grad, embedded = call(
         score_kernel,
-        [shape((slots, nodes), BF16), shape((slots, width), BF16)],
+        [
+            shape((slots, nodes), BF16),
+            shape((slots, width), BF16),
+            shape((nodes, width), F32),
+            jax.ShapeDtypeStruct((nodes, width), BF16),
+        ],
         got,
         embed,
         live,
+        pairs,
         scale=scale,
+        scratch=[pltpu.SemaphoreType.DMA((1,))],
     )
     terms = exchanged(back, peers)
-    [out] = call(final_kernel, [jax.ShapeDtypeStruct((nodes, width), BF16)], spread, terms, weight, got, grad)
+    [out] = call(final_kernel, [shape((nodes, width), BF16)], spread, terms, weight, got, grad)
     return (embedded, out)
 
 

time: 66.5 us -> 65.8 us (0.989)
  blocking collectives: 20 us -> 45.6 us
  waiting for transfers between devices: 15.7 us -> 1.26 us
  starting transfers between devices: 21.5 us -> 11 us
  Pallas kernels: 7.5 us -> 6.22 us
    all_to_all x1 -> x2, blocking collectives: 20 us -> 45.6 us  [exchanged(): lax.all_to_all(block, 'wide', split_axis=0, concat_axis=0, tiled=True)]
    all_to_all x1 -> x0, waiting for transfers between devices: 15.7 us -> none  [exchanged(): lax.all_to_all(block, 'wide', split_axis=0, concat_axis=0, tiled=True)]
    all_to_all x1 -> x0, starting transfers between devices: 8.69 us -> none  [exchanged(): lax.all_to_all(block, 'wide', split_axis=0, concat_axis=0, tiled=True)]
    ppermute x2, starting transfers between devices: 12.9 us -> 11 us  [passed_along(): return lax.ppermute(block, axis, route)]
    pallas_call x6, Pallas kernels: 7.5 us -> 6.22 us  [call(): pl.pallas_call(functools.partial(kernel, **static) if static else kernel,...]
    ppermute x2, waiting for transfers between devices: 0.01 us -> 1.26 us  [passed_along(): return lax.ppermute(block, axis, route)]
  transfers between devices with their start and end apart: 3 -> 2, of which waited for: 1 -> 1; matrix products, arithmetic and copies ran while one was open for 0% -> 0% of each run, Pallas kernels for 3% -> 3%
where the time goes in v4:
time: 65.8 us; the launch traced here: 65.5 us
  blocking collectives  45.6 us (69%)
  starting transfers between devices  11 us (17%)
  Pallas kernels  6.22 us (9%)
  waiting for transfers between devices  1.26 us (2%)
  between operations  0.73 us (1%)
  local copies, waits for them, and re-layouts  0.72 us (1%)
    all_to_all x2, blocking collectives, exchanged(): lax.all_to_all(block, 'wide', split_axis=0, concat_axis=0, tiled=True)  45.6 us
    ppermute x2, starting transfers between devices, passed_along(): return lax.ppermute(block, axis, route)  11 us
    pallas_call x6, Pallas kernels, call(): pl.pallas_call(functools.partial(kernel, **static) if static else kernel,...  6.22 us
  transfers between devices with their start and end apart: 2, of which 1 were waited for; matrix products, arithmetic and copies ran while one was open for 0% of the time, Pallas kernels for 3%

profile of v4, /device:TPU:7, one launch (start us, length us, event | category | flops | bytes accessed | tf_op | source)
XLA Modules:
  0.0 65.5 jit_solution(9251322704786531706)
XLA Ops:
  0.6 0.0 copy-start.1
  0.6 1.9 %head_kernel.1 = (s32[1,2,64]{2,1,0:T(2,128)}, s32[16,32]{1,0:T(8,128)S(1)}, bf16[256,512]{1,0:T(8,128)(2,1)S(1)}, s32[16,256]{1,0:T(8,128)S(1)}, s32[2,256]{1,0...) custom-call(s32[1,2,64]{2,1,0:T(2,128)} %refs_0_.3, ...), custom_call_target="tpu_custom_call" | custom-call | tf_op jit(solution)/shard_map/head_kernel/pallas_call | solution.py:22
  2.5 4.0 %collective-permute-start = (bf16[64,512]{1,0:T(8,128)(2,1)S(1)}, bf16[64,512]{1,0:T(8,128)(2,1)S(1)}, u32[]{:S(2)}, u32[]{:S(2)}) collective-permute-start(bf16[64,512]{1,0:T(8,128)(2,1)S(1)} %get-tuple-element.37), channel_id=1, source_target_pairs={{0,16},{16,32},{32,48},{48,64},{64,80},{80,96},{96,112},{112,128},... | collective-permute-start | bytes 196616 | tf_op jit(solution)/shard_map/ppermute | solution.py:155
  6.5 0.0 copy-done.1
  6.6 2.0 %own_kernel.2 = (f32[256,512]{1,0:T(8,128)S(1)}, f32[256,512]{1,0:T(8,128)S(1)}, bf16[256,128]{1,0:T(8,128)(2,1)S(1)}, f32[256,1]{1,0:T(8,128)S(1)}, bf16[512,25...) custom-call(bf16[512,512]{1,0:T(8,128)(2,1)} %refs_0_.5, ...), custom_call_target="tpu_custom_call" | custom-call | tf_op jit(solution)/shard_map/own_kernel/pallas_call | solution.py:22
  8.6 0.0 copy-start
  8.6 7.0 %collective-permute-start.1 = (bf16[64,512]{1,0:T(8,128)(2,1)S(1)}, bf16[64,512]{1,0:T(8,128)(2,1)S(1)}, u32[]{:S(2)}, u32[]{:S(2)}) collective-permute-start(bf16[64,512]{1,0:T(8,128)(2,1)S(1)} %get-tuple-element.50), channel_id=1, source_target_pairs={{16,0},{32,16},{48,32},{64,48},{80,64},{96,80},{112,96},{128,112},... | collective-permute-start | bytes 196616 | tf_op jit(solution)/shard_map/ppermute | solution.py:155
  15.6 0.0 collective-permute-done.below_ref
  15.7 1.3 %collective-permute-done.1.above_ref = bf16[64,512]{1,0:T(8,128)(2,1)S(1)} collective-permute-done((bf16[64,512]{1,0:T(8,128)(2,1)S(1)}, bf16[64,512]{1,0:T(8,128)(2,1)S(1)}, u32[]{:S(2)}, u32[]{:S(2)}) %collective-permute-start.1) | collective-permute-done | bytes 65568 | tf_op jit(solution)/shard_map/ppermute | solution.py:155
  16.9 0.0 copy-done
  16.9 0.8 %embed_kernel.1 = (bf16[256,512]{1,0:T(8,128)(2,1)S(1)}, bf16[512,512]{1,0:T(8,128)(2,1)S(1)}) custom-call(bf16[64,512]{1,0:T(8,128)(2,1)S(1)} %collective-permute-done.below_ref, bf16[64,512]{1,0:T(8,128)(2,1)S(1)} %collective-permute-done.1.above_ref, bf16[256,128]{1,0:T(8,128)(2,1)S(1)} %get-tuple-element.58.counts_ref, ...), custom_call_target="tpu_custom_call" | custom-call | tf_op jit(solution)/shard_map/embed_kernel/pallas_call | solution.py:22
  17.7 25.6 %all_to_all.10 = bf16[16,32,512]{2,1,0:T(8,128)(2,1)S(1)} all-to-all(bf16[16,32,512]{2,1,0:T(8,128)(2,1)S(1)} %bitcast.10), channel_id=1, replica_groups=mesh['dom'=32,'wide'=16] {'wide'}, dimensions={0} | all-to-all | bytes 1048576 | tf_op jit(solution)/shard_map/all_to_all | solution.py:160
  43.3 1.0 %score_kernel.1 = (bf16[512,256]{1,0:T(8,128)(2,1)S(1)}, bf16[512,512]{1,0:T(8,128)(2,1)S(1)}, f32[256,512]{1,0:T(8,128)S(1)}, bf16[256,512]{1,0:T(8,128)(2,1)}) custom-call(bf16[512,512]{1,0:T(8,128)(2,1)S(1)} %bitcast.7, bf16[256,512]{1,0:T(8,128)(2,1)S(1)} %get-tuple-element.64.embed_ref, bf16[512,256]{1,0:T(8,128)(2,1)S(1)} %get-tuple-element.65.live_ref, ...), custom_call_target="tpu_custom_call" | custom-call | tf_op jit(solution)/shard_map/score_kernel/pallas_call | solution.py:22
  44.4 20.0 %all_to_all.11 = bf16[16,32,512]{2,1,0:T(8,128)(2,1)S(1)} all-to-all(bf16[16,32,512]{2,1,0:T(8,128)(2,1)S(1)} %bitcast.11), channel_id=1, replica_groups=mesh['dom'=32,'wide'=16] {'wide'}, dimensions={0} | all-to-all | bytes 1048576 | tf_op jit(solution)/shard_map/all_to_all | solution.py:160
  64.4 0.5 final_kernel.1
  64.8 0.7 %copy.24 = bf16[256,512]{1,0:T(8,128)(2,1)} copy(bf16[256,512]{1,0:T(8,128)(2,1)S(1)} %final_kernel.1) | data formatting | bytes 524288
  (1 shorter events, 0.0 us)
Async XLA Ops:
  0.6 5.9 %copy-start.1 = (s32[16,32,8]{1,2,0:T(8,128)S(1)}, s32[16,32,8]{1,2,0:T(8,128)}, u32[]{:S(2)}) copy-start(s32[16,32,8]{1,2,0:T(8,128)} %param.14) | copy-start | bytes 49156
  2.5 13.1 %collective-permute-start = (bf16[64,512]{1,0:T(8,128)(2,1)S(1)}, bf16[64,512]{1,0:T(8,128)(2,1)S(1)}, u32[]{:S(2)}, u32[]{:S(2)}) collective-permute-start(bf16[64,512]{1,0:T(8,128)(2,1)S(1)} %get-tuple-element.37), channel_id=1, source_target_pairs={{0,16},{16,32},{32,48},{48,64},{64,80},{80,96},{96,112},{112,128},... | collective-permute-start | bytes 196616 | tf_op jit(solution)/shard_map/ppermute | solution.py:155
  8.6 8.3 %copy-start = (bf16[512,512]{1,0:T(8,128)(2,1)S(1)}, bf16[512,512]{1,0:T(8,128)(2,1)}, u32[]{:S(2)}) copy-start(bf16[512,512]{1,0:T(8,128)(2,1)} %w_neigh_ref.1) | copy-start | bytes 1572868
  8.6 8.3 %collective-permute-start.1 = (bf16[64,512]{1,0:T(8,128)(2,1)S(1)}, bf16[64,512]{1,0:T(8,128)(2,1)S(1)}, u32[]{:S(2)}, u32[]{:S(2)}) collective-permute-start(bf16[64,512]{1,0:T(8,128)(2,1)S(1)} %get-tuple-element.50), channel_id=1, source_target_pairs={{16,0},{32,16},{48,32},{64,48},{80,64},{96,80},{112,96},{128,112},... | collective-permute-start | bytes 196616 | tf_op jit(solution)/shard_map/ppermute | solution.py:155

commit v5 on v4

--- a/solution.py
+++ b/solution.py
@@ -70,48 +70,45 @@
     return total
 
 
-def head_kernel(*refs):
-    fetched = 5
-    held, (pick_ref, up_ref, down_ref, arrived) = refs[fetched : 2 * fetched], refs[2 * fetched :]
-    copies = fetch(zip(refs[:fetched], held), arrived)
-    lists_ref, anchors_ref, features_ref = held[:3]
+def head_kernel(lists_hbm, features_hbm, lists_ref, features_ref, up_ref, down_ref, arrived):
+    lists_here, features_here = fetch(((lists_hbm, lists_ref), (features_hbm, features_ref)), arrived)
+    lists_here.wait()
     nodes = features_ref.shape[0]
-    copies[0].wait()
     onehots = [row_counts(lists_ref[0, side : side + 1, :], nodes).astype(BF16) for side in range(2)]
-    copies[1].wait()
-    slots = jnp.concatenate([anchors_ref[j : j + 1, :] for j in range(anchors_ref.shape[0])], axis=1)
-    pick_ref[...] = column_counts(slots.T, nodes)
-    copies[2].wait()
+    features_here.wait()
     for onehot, out in zip(onehots, (up_ref, down_ref)):
         out[...] = dot_tn(onehot, features_ref[...]).astype(BF16)
-    for copy in copies[3:]:
-        copy.wait()
 
 
 def own_kernel(*refs, turn, made):
-    w_self_hbm, features_ref, neighbors_ref, negatives_ref, positives_ref, anchors_ref = refs[:6]
-    own_ref, summed_ref, counts_ref, degree_ref, live_ref, spread_ref, pairs_ref = refs[len(refs) - made - 2 : -2]
-    w_self_ref, arrived = refs[-2:]
+    given, (features_ref, negatives_ref) = refs[:4], refs[4:6]
+    outs, held, arrived = refs[len(refs) - made - 5 : -5], refs[-5:-1], refs[-1]
+    own_ref, summed_ref, counts_ref, degree_ref, pick_ref, live_ref, spread_ref, pairs_ref = outs
+    neighbors_ref, anchors_ref, positives_ref, w_self_ref = held
 
     @pl.when(waits_long() if turn == 0 else jnp.logical_not(waits_long()))
     def _():
-        [copy] = fetch(((w_self_hbm, w_self_ref),), arrived)
+        copies = fetch(zip(given, held), arrived)
         features = features_ref[...]
         nodes = features.shape[0]
         edge = counts_ref.shape[1]
         peers = negatives_ref.shape[0]
+        slots = jnp.concatenate([negatives_ref[j] for j in range(peers)], axis=1)
+        live_ref[...] = column_counts(slots.T, nodes)
+        copies[0].wait()
         counts = column_counts(neighbors_ref[...].T, nodes + edge)
         degree_ref[...] = jnp.sum(counts.astype(F32), axis=1, keepdims=True)
         counts_ref[...] = counts[:, nodes:]
         summed_ref[...] = dot(counts[:, :nodes], features)
-        slots = jnp.concatenate([negatives_ref[j] for j in range(peers)], axis=1)
-        live_ref[...] = column_counts(slots.T, nodes)
+        copies[1].wait()
         anchors = jnp.concatenate([anchors_ref[j : j + 1, :] for j in range(peers)], axis=1)
+        pick_ref[...] = column_counts(anchors.T, nodes)
         spread_ref[...] = row_counts(anchors, nodes).astype(BF16)
+        copies[2].wait()
         first = row_counts(positives_ref[0:1, :], nodes).astype(BF16)
         second = row_counts(positives_ref[1:2, :], nodes).astype(BF16)
         pairs_ref[...] = dot_nt(first, second) + dot_nt(second, first)
-        copy.wait()
+        copies[3].wait()
         own_ref[...] = dot(features, w_self_ref[...])
 
 
@@ -166,32 +163,42 @@
     peers, anch = anchors.shape
     slots = peers * anch
     edge = boundary.shape[2]
-    given = (boundary, anchors, features, neighbors.T, positives.T)
-    _, anchors, features, neighbors, positives, pick, up, down = call(
+    _, features, up, down = call(
         head_kernel,
-        [shape(x.shape, x.dtype) for x in given] + [shape((slots, nodes), BF16)] + [shape((edge, width), BF16)] * 2,
-        *given,
-        from_hbm=len(given),
-        scratch=[pltpu.SemaphoreType.DMA((len(given),))],
-    )
-    local = (w_self, features, neighbors, negatives.transpose(0, 2, 1), positives, anchors)
+        [shape(boundary.shape, boundary.dtype), shape((nodes, width), BF16)] + [shape((edge, width), BF16)] * 2,
+        boundary,
+        features,
+        from_hbm=2,
+        scratch=[pltpu.SemaphoreType.DMA((2,))],
+    )
+    given = (neighbors.T, anchors, positives.T, w_self)
+    local = given + (features, negatives.transpose(0, 2, 1))
     made = [
         shape((nodes, width), F32),
         shape((nodes, width), F32),
         shape((nodes, 2 * edge), BF16),
         shape((nodes, 1), F32),
         shape((slots, nodes), BF16),
+        shape((slots, nodes), BF16),
         shape((nodes, slots), BF16),
         shape((nodes, nodes), F32),
     ]
     below = passed_along(up, "dom", 1)
-    room = [pltpu.VMEM(w_self.shape, BF16), pltpu.SemaphoreType.DMA((1,))]
-    early = call(own_kernel, made, *local, from_hbm=1, scratch=room, turn=0, made=len(made))
+    room = [pltpu.VMEM(x.shape, x.dtype) for x in given] + [pltpu.SemaphoreType.DMA((len(given),))]
+    early = call(own_kernel, made, *local, from_hbm=len(given), scratch=room, turn=0, made=len(made))
     down, early = lax.optimization_barrier((down, early))
     above = passed_along(down, "dom", -1)
     aliases = {len(local) + n: n for n in range(len(made))}
-    own, summed, counts, degree, live, spread, pairs = call(
-        own_kernel, made, *local, *early, from_hbm=1, scratch=room, aliases=aliases, turn=1, made=len(made)
+    own, summed, counts, degree, pick, live, spread, pairs = call(
+        own_kernel,
+        made,
+        *local,
+        *early,
+        from_hbm=len(given),
+        scratch=room,
+        aliases=aliases,
+        turn=1,
+        made=len(made),
     )
     embed, rows = call(
         embed_kernel,

time: 65.8 us -> 65.6 us (level)
  transfers between devices with their start and end apart: 2 -> 2, of which waited for: 1 -> 1; matrix products, arithmetic and copies ran while one was open for 0% -> 0% of each run, Pallas kernels for 3% -> 4%
where the time goes in v5:
time: 65.6 us; the launch traced here: 65.2 us
  blocking collectives  45.6 us (70%)
  starting transfers between devices  10.7 us (16%)
  Pallas kernels  6.25 us (10%)
  waiting for transfers between devices  1.23 us (2%)
  between operations  0.73 us (1%)
  local copies, waits for them, and re-layouts  0.72 us (1%)
    all_to_all x2, blocking collectives, exchanged(): lax.all_to_all(block, 'wide', split_axis=0, concat_axis=0, tiled=True)  45.6 us
    ppermute x2, starting transfers between devices, passed_along(): return lax.ppermute(block, axis, route)  10.7 us
    pallas_call x6, Pallas kernels, call(): pl.pallas_call(functools.partial(kernel, **static) if static else kernel,...  6.25 us
  transfers between devices with their start and end apart: 2, of which 1 were waited for; matrix products, arithmetic and copies ran while one was open for 0% of the time, Pallas kernels for 4%

profile of v5, /device:TPU:7, one launch (start us, length us, event | category | flops | bytes accessed | tf_op | source)
XLA Modules:
  0.0 65.2 jit_solution(2017590882379626553)
XLA Ops:
  0.6 0.0 copy-start.1
  0.6 1.6 %head_kernel.1 = (s32[1,2,64]{2,1,0:T(2,128)}, bf16[256,512]{1,0:T(8,128)(2,1)S(1)}, bf16[64,512]{1,0:T(8,128)(2,1)S(1)}, bf16[64,512]{1,0:T(8,128)(2,1)S(1)}) custom-call(s32[1,2,64]{2,1,0:T(2,128)} %lists_hbm.1, bf16[256,512]{1,0:T(8,128)(2,1)} %features_hbm.1), custom_call_target="tpu_custom_call" | custom-call | tf_op jit(solution)/shard_map/head_kernel/pallas_call | solution.py:22
  2.2 4.0 %collective-permute-start = (bf16[64,512]{1,0:T(8,128)(2,1)S(1)}, bf16[64,512]{1,0:T(8,128)(2,1)S(1)}, u32[]{:S(2)}, u32[]{:S(2)}) collective-permute-start(bf16[64,512]{1,0:T(8,128)(2,1)S(1)} %get-tuple-element.36), channel_id=1, source_target_pairs={{0,16},{16,32},{32,48},{48,64},{64,80},{80,96},{96,112},{112,128},... | collective-permute-start | bytes 196616 | tf_op jit(solution)/shard_map/ppermute | solution.py:152
  6.2 0.0 copy-done.1
  6.2 2.4 %own_kernel.2 = (f32[256,512]{1,0:T(8,128)S(1)}, f32[256,512]{1,0:T(8,128)S(1)}, bf16[256,128]{1,0:T(8,128)(2,1)S(1)}, f32[256,1]{1,0:T(8,128)S(1)}, bf16[512,25...) custom-call(s32[16,256]{1,0:T(8,128)} %bitcast.14, ...), custom_call_target="tpu_custom_call" | custom-call | tf_op jit(solution)/shard_map/own_kernel/pallas_call | solution.py:22
  8.6 0.0 copy-start
  8.6 6.7 %collective-permute-start.1 = (bf16[64,512]{1,0:T(8,128)(2,1)S(1)}, bf16[64,512]{1,0:T(8,128)(2,1)S(1)}, u32[]{:S(2)}, u32[]{:S(2)}) collective-permute-start(bf16[64,512]{1,0:T(8,128)(2,1)S(1)} %get-tuple-element.47), channel_id=1, source_target_pairs={{16,0},{32,16},{48,32},{64,48},{80,64},{96,80},{112,96},{128,112},... | collective-permute-start | bytes 196616 | tf_op jit(solution)/shard_map/ppermute | solution.py:152
  15.3 0.1 own_kernel.3
  15.4 0.0 collective-permute-done.below_ref
  15.4 1.2 %collective-permute-done.1.above_ref = bf16[64,512]{1,0:T(8,128)(2,1)S(1)} collective-permute-done((bf16[64,512]{1,0:T(8,128)(2,1)S(1)}, bf16[64,512]{1,0:T(8,128)(2,1)S(1)}, u32[]{:S(2)}, u32[]{:S(2)}) %collective-permute-start.1) | collective-permute-done | bytes 65568 | tf_op jit(solution)/shard_map/ppermute | solution.py:152
  16.6 0.0 copy-done
  16.6 0.7 %embed_kernel.1 = (bf16[256,512]{1,0:T(8,128)(2,1)S(1)}, bf16[512,512]{1,0:T(8,128)(2,1)S(1)}) custom-call(bf16[64,512]{1,0:T(8,128)(2,1)S(1)} %collective-permute-done.below_ref, bf16[64,512]{1,0:T(8,128)(2,1)S(1)} %collective-permute-done.1.above_ref, bf16[256,128]{1,0:T(8,128)(2,1)S(1)} %get-tuple-element.56.counts_ref, ...), custom_call_target="tpu_custom_call" | custom-call | tf_op jit(solution)/shard_map/embed_kernel/pallas_call | solution.py:22
  17.4 25.6 %all_to_all.10 = bf16[16,32,512]{2,1,0:T(8,128)(2,1)S(1)} all-to-all(bf16[16,32,512]{2,1,0:T(8,128)(2,1)S(1)} %bitcast.10), channel_id=1, replica_groups=mesh['dom'=32,'wide'=16] {'wide'}, dimensions={0} | all-to-all | bytes 1048576 | tf_op jit(solution)/shard_map/all_to_all | solution.py:157
  43.0 1.0 %score_kernel.1 = (bf16[512,256]{1,0:T(8,128)(2,1)S(1)}, bf16[512,512]{1,0:T(8,128)(2,1)S(1)}, f32[256,512]{1,0:T(8,128)S(1)}, bf16[256,512]{1,0:T(8,128)(2,1)}) custom-call(bf16[512,512]{1,0:T(8,128)(2,1)S(1)} %bitcast.7, bf16[256,512]{1,0:T(8,128)(2,1)S(1)} %get-tuple-element.62.embed_ref, bf16[512,256]{1,0:T(8,128)(2,1)S(1)} %get-tuple-element.63.live_ref, ...), custom_call_target="tpu_custom_call" | custom-call | tf_op jit(solution)/shard_map/score_kernel/pallas_call | solution.py:22
  44.1 20.0 %all_to_all.11 = bf16[16,32,512]{2,1,0:T(8,128)(2,1)S(1)} all-to-all(bf16[16,32,512]{2,1,0:T(8,128)(2,1)S(1)} %bitcast.11), channel_id=1, replica_groups=mesh['dom'=32,'wide'=16] {'wide'}, dimensions={0} | all-to-all | bytes 1048576 | tf_op jit(solution)/shard_map/all_to_all | solution.py:157
  64.1 0.5 final_kernel.1
  64.5 0.7 %copy.26 = bf16[256,512]{1,0:T(8,128)(2,1)} copy(bf16[256,512]{1,0:T(8,128)(2,1)S(1)} %final_kernel.1) | data formatting | bytes 524288
Async XLA Ops:
  0.6 5.6 %copy-start.1 = (s32[16,32,8]{1,2,0:T(8,128)S(1)}, s32[16,32,8]{1,2,0:T(8,128)}, u32[]{:S(2)}) copy-start(s32[16,32,8]{1,2,0:T(8,128)} %param.14) | copy-start | bytes 49156
  2.2 13.2 %collective-permute-start = (bf16[64,512]{1,0:T(8,128)(2,1)S(1)}, bf16[64,512]{1,0:T(8,128)(2,1)S(1)}, u32[]{:S(2)}, u32[]{:S(2)}) collective-permute-start(bf16[64,512]{1,0:T(8,128)(2,1)S(1)} %get-tuple-element.36), channel_id=1, source_target_pairs={{0,16},{16,32},{32,48},{48,64},{64,80},{80,96},{96,112},{112,128},... | collective-permute-start | bytes 196616 | tf_op jit(solution)/shard_map/ppermute | solution.py:152
  8.6 8.0 %copy-start = (bf16[512,512]{1,0:T(8,128)(2,1)S(1)}, bf16[512,512]{1,0:T(8,128)(2,1)}, u32[]{:S(2)}) copy-start(bf16[512,512]{1,0:T(8,128)(2,1)} %w_neigh_ref.1) | copy-start | bytes 1572868
  8.6 8.0 %collective-permute-start.1 = (bf16[64,512]{1,0:T(8,128)(2,1)S(1)}, bf16[64,512]{1,0:T(8,128)(2,1)S(1)}, u32[]{:S(2)}, u32[]{:S(2)}) collective-permute-start(bf16[64,512]{1,0:T(8,128)(2,1)S(1)} %get-tuple-element.47), channel_id=1, source_target_pairs={{16,0},{32,16},{48,32},{64,48},{80,64},{96,80},{112,96},{128,112},... | collective-permute-start | bytes 196616 | tf_op jit(solution)/shard_map/ppermute | solution.py:152

commit v6 on v5

--- a/solution.py
+++ b/solution.py
@@ -134,9 +134,12 @@
     copy.wait()
 
 
-def final_kernel(spread_ref, terms_ref, weight_ref, got_ref, grad_ref, out_ref):
+def final_kernel(spread_ref, terms_ref, weight_ref, got_ref, grad_ref, out_ref, held_ref, sent):
     total = grad_ref[...] + dot_tn(weight_ref[...], got_ref[...]) + dot(spread_ref[...], terms_ref[...])
-    out_ref[...] = total.astype(BF16)
+    held_ref[...] = total.astype(BF16)
+    copy = pltpu.make_async_copy(held_ref, out_ref, sent.at[0])
+    copy.start()
+    copy.wait()
 
 
 ROW = 8
@@ -229,7 +232,16 @@
         scratch=[pltpu.SemaphoreType.DMA((1,))],
     )
     terms = exchanged(back, peers)
-    [out] = call(final_kernel, [shape((nodes, width), BF16)], spread, terms, weight, got, grad)
+    [out] = call(
+        final_kernel,
+        [jax.ShapeDtypeStruct((nodes, width), BF16)],
+        spread,
+        terms,
+        weight,
+        got,
+        grad,
+        scratch=[pltpu.VMEM((nodes, width), BF16), pltpu.SemaphoreType.DMA((1,))],
+    )
     return (embedded, out)
 
 

time: 65.6 us -> 65.6 us (level)
  Pallas kernels: 6.25 us -> 6.97 us
  local copies, waits for them, and re-layouts: 0.72 us -> 0.01 us
    pallas_call x6, Pallas kernels: 6.25 us -> 6.97 us  [call(): pl.pallas_call(functools.partial(kernel, **static) if static else kernel,...]
    unnamed x5 -> x4, local copies, waits for them, and re-layouts: 0.72 us -> 0.01 us
where the time goes in v6:
time: 65.6 us; the launch traced here: 65.2 us
  blocking collectives  45.6 us (70%)
  starting transfers between devices  10.7 us (16%)
  Pallas kernels  6.97 us (11%)
  waiting for transfers between devices  1.23 us (2%)
  between operations  0.72 us (1%)
    all_to_all x2, blocking collectives, exchanged(): lax.all_to_all(block, 'wide', split_axis=0, concat_axis=0, tiled=True)  45.6 us
    ppermute x2, starting transfers between devices, passed_along(): return lax.ppermute(block, axis, route)  10.7 us
    pallas_call x6, Pallas kernels, call(): pl.pallas_call(functools.partial(kernel, **static) if static else kernel,...  6.97 us
  transfers between devices with their start and end apart: 2, of which 1 were waited for; matrix products, arithmetic and copies ran while one was open for 0% of the time, Pallas kernels for 4%

profile of v6, /device:TPU:7, one launch (start us, length us, event | category | flops | bytes accessed | tf_op | source)
XLA Modules:
  0.0 65.2 jit_solution(1382596902494867778)
XLA Ops:
  0.6 0.0 copy-start.1
  0.6 1.6 %head_kernel.1 = (s32[1,2,64]{2,1,0:T(2,128)}, bf16[256,512]{1,0:T(8,128)(2,1)S(1)}, bf16[64,512]{1,0:T(8,128)(2,1)S(1)}, bf16[64,512]{1,0:T(8,128)(2,1)S(1)}) custom-call(s32[1,2,64]{2,1,0:T(2,128)} %lists_hbm.1, bf16[256,512]{1,0:T(8,128)(2,1)} %features_hbm.1), custom_call_target="tpu_custom_call" | custom-call | tf_op jit(solution)/shard_map/head_kernel/pallas_call | solution.py:22
  2.2 4.0 %collective-permute-start = (bf16[64,512]{1,0:T(8,128)(2,1)S(1)}, bf16[64,512]{1,0:T(8,128)(2,1)S(1)}, u32[]{:S(2)}, u32[]{:S(2)}) collective-permute-start(bf16[64,512]{1,0:T(8,128)(2,1)S(1)} %get-tuple-element.36), channel_id=1, source_target_pairs={{0,16},{16,32},{32,48},{48,64},{64,80},{80,96},{96,112},{112,128},... | collective-permute-start | bytes 196616 | tf_op jit(solution)/shard_map/ppermute | solution.py:155
  6.2 0.0 copy-done.1
  6.2 2.4 %own_kernel.2 = (f32[256,512]{1,0:T(8,128)S(1)}, f32[256,512]{1,0:T(8,128)S(1)}, bf16[256,128]{1,0:T(8,128)(2,1)S(1)}, f32[256,1]{1,0:T(8,128)S(1)}, bf16[512,25...) custom-call(s32[16,256]{1,0:T(8,128)} %bitcast.14, ...), custom_call_target="tpu_custom_call" | custom-call | tf_op jit(solution)/shard_map/own_kernel/pallas_call | solution.py:22
  8.6 0.0 copy-start
  8.6 6.7 %collective-permute-start.1 = (bf16[64,512]{1,0:T(8,128)(2,1)S(1)}, bf16[64,512]{1,0:T(8,128)(2,1)S(1)}, u32[]{:S(2)}, u32[]{:S(2)}) collective-permute-start(bf16[64,512]{1,0:T(8,128)(2,1)S(1)} %get-tuple-element.47), channel_id=1, source_target_pairs={{16,0},{32,16},{48,32},{64,48},{80,64},{96,80},{112,96},{128,112},... | collective-permute-start | bytes 196616 | tf_op jit(solution)/shard_map/ppermute | solution.py:155
  15.3 0.1 own_kernel.3
  15.4 0.0 collective-permute-done.below_ref
  15.4 1.2 %collective-permute-done.1.above_ref = bf16[64,512]{1,0:T(8,128)(2,1)S(1)} collective-permute-done((bf16[64,512]{1,0:T(8,128)(2,1)S(1)}, bf16[64,512]{1,0:T(8,128)(2,1)S(1)}, u32[]{:S(2)}, u32[]{:S(2)}) %collective-permute-start.1) | collective-permute-done | bytes 65568 | tf_op jit(solution)/shard_map/ppermute | solution.py:155
  16.6 0.0 copy-done
  16.6 0.7 %embed_kernel.1 = (bf16[256,512]{1,0:T(8,128)(2,1)S(1)}, bf16[512,512]{1,0:T(8,128)(2,1)S(1)}) custom-call(bf16[64,512]{1,0:T(8,128)(2,1)S(1)} %collective-permute-done.below_ref, bf16[64,512]{1,0:T(8,128)(2,1)S(1)} %collective-permute-done.1.above_ref, bf16[256,128]{1,0:T(8,128)(2,1)S(1)} %get-tuple-element.56.counts_ref, ...), custom_call_target="tpu_custom_call" | custom-call | tf_op jit(solution)/shard_map/embed_kernel/pallas_call | solution.py:22
  17.4 25.6 %all_to_all.10 = bf16[16,32,512]{2,1,0:T(8,128)(2,1)S(1)} all-to-all(bf16[16,32,512]{2,1,0:T(8,128)(2,1)S(1)} %bitcast.10), channel_id=1, replica_groups=mesh['dom'=32,'wide'=16] {'wide'}, dimensions={0} | all-to-all | bytes 1048576 | tf_op jit(solution)/shard_map/all_to_all | solution.py:160
  43.0 1.0 %score_kernel.1 = (bf16[512,256]{1,0:T(8,128)(2,1)S(1)}, bf16[512,512]{1,0:T(8,128)(2,1)S(1)}, f32[256,512]{1,0:T(8,128)S(1)}, bf16[256,512]{1,0:T(8,128)(2,1)}) custom-call(bf16[512,512]{1,0:T(8,128)(2,1)S(1)} %bitcast.7, bf16[256,512]{1,0:T(8,128)(2,1)S(1)} %get-tuple-element.62.embed_ref, bf16[512,256]{1,0:T(8,128)(2,1)S(1)} %get-tuple-element.63.live_ref, ...), custom_call_target="tpu_custom_call" | custom-call | tf_op jit(solution)/shard_map/score_kernel/pallas_call | solution.py:22
  44.1 20.0 %all_to_all.11 = bf16[16,32,512]{2,1,0:T(8,128)(2,1)S(1)} all-to-all(bf16[16,32,512]{2,1,0:T(8,128)(2,1)S(1)} %bitcast.11), channel_id=1, replica_groups=mesh['dom'=32,'wide'=16] {'wide'}, dimensions={0} | all-to-all | bytes 1048576 | tf_op jit(solution)/shard_map/all_to_all | solution.py:160
  64.1 1.2 %final_kernel.1 = bf16[256,512]{1,0:T(8,128)(2,1)} custom-call(bf16[256,512]{1,0:T(8,128)(2,1)S(1)} %get-tuple-element.66.spread_ref, bf16[512,512]{1,0:T(8,128)(2,1)S(1)} %bitcast.9, bf16[512,256]{1,0:T(8,128)(2,1)S(1)} %get-tuple-element.68.weight_ref, bf16[512,512]{1,0:T(8,128)(2,1)S(1)} %bitcast.8, f32[256,512]{1,0:T(8,128)S(1)} %get-tuple-element.69.grad_ref), custom_call_target="tpu_custom_call" | custom-call | tf_op jit(solution)/shard_map/final_kernel/pallas_call | solution.py:22
Async XLA Ops:
  0.6 5.6 %copy-start.1 = (s32[16,32,8]{1,2,0:T(8,128)S(1)}, s32[16,32,8]{1,2,0:T(8,128)}, u32[]{:S(2)}) copy-start(s32[16,32,8]{1,2,0:T(8,128)} %param.14) | copy-start | bytes 49156
  2.2 13.2 %collective-permute-start = (bf16[64,512]{1,0:T(8,128)(2,1)S(1)}, bf16[64,512]{1,0:T(8,128)(2,1)S(1)}, u32[]{:S(2)}, u32[]{:S(2)}) collective-permute-start(bf16[64,512]{1,0:T(8,128)(2,1)S(1)} %get-tuple-element.36), channel_id=1, source_target_pairs={{0,16},{16,32},{32,48},{48,64},{64,80},{80,96},{96,112},{112,128},... | collective-permute-start | bytes 196616 | tf_op jit(solution)/shard_map/ppermute | solution.py:155
  8.6 8.0 %copy-start = (bf16[512,512]{1,0:T(8,128)(2,1)S(1)}, bf16[512,512]{1,0:T(8,128)(2,1)}, u32[]{:S(2)}) copy-start(bf16[512,512]{1,0:T(8,128)(2,1)} %w_neigh_ref.1) | copy-start | bytes 1572868
  8.6 8.0 %collective-permute-start.1 = (bf16[64,512]{1,0:T(8,128)(2,1)S(1)}, bf16[64,512]{1,0:T(8,128)(2,1)S(1)}, u32[]{:S(2)}, u32[]{:S(2)}) collective-permute-start(bf16[64,512]{1,0:T(8,128)(2,1)S(1)} %get-tuple-element.47), channel_id=1, source_target_pairs={{16,0},{32,16},{48,32},{64,48},{80,64},{96,80},{112,96},{128,112},... | collective-permute-start | bytes 196616 | tf_op jit(solution)/shard_map/ppermute | solution.py:155
